TPU v7x, 32 devices: a whole 2x2x4 slice. The times are simulated.
32 devices in a mesh: gx: 4 (over y, x), gy: 4 (over z), gz: 2 (over core).
Axes of the slice: x: 2, y: 2, z: 4, core: 2. Of those that a mesh axis runs over, the one named last changes fastest.
Arguments:
- positions: float32 [2048, 3, 128], P(('gx', 'gy', 'gz')), may hold values from 0 to 1
- charges: float32 [2048, 128], P(('gx', 'gy', 'gz')), may hold values from -0.18 to 0.18
- counts: int32 [2048], P(('gx', 'gy', 'gz')), may hold values from 1 to 128
- up_inverse: float32 [64, 64], replicated, may hold values from -0.09375 to 0.09375
- down_inverse: float32 [64, 64], replicated, may hold values from -0.09375 to 0.09375
- inner_surface: float32 [3, 64], replicated, may hold values from 0.15 to 0.85
- outer_surface: float32 [3, 64], replicated, may hold values from -1 to 2, as said below
Outputs:
- potential: float32 [2048, 128], P(('gx', 'gy', 'gz'))
Inputs may be any that keep to these rules, and one draw needn't show every extreme that they name: `outer_surface`: each point lies on the boundary of the cube [-1, 2]^3.
All inputs are finite; a program needn't handle non-finite values.
Results may differ from a plain program's by a relative error of at most 0.0003.
Values sent between devices are 32-bit elements; how exact they have to be, the bound alone decides.
A program may use at most 64 MiB of HBM per device.

v0:
```python
from functools import partial
import math

import jax
import jax.numpy as jnp
from jax import lax
from jax.sharding import PartitionSpec as P

CX = 4
CY = 4
CZ = 4
PTS = 128
TERMS = 64


SOFTEN = 0.0025
EXACT_DOTS = lax.Precision.HIGHEST


def from_partner(value, axis, stride):
    mask = 2**stride
    pairs = [(source, source ^ mask) for source in range(lax.axis_size(axis))]
    return lax.ppermute(value, axis, pairs)


def kernel(square):
    return 1.0 / jnp.sqrt(square + SOFTEN)


def leaf_blocks(function, arrays, block_size):
    leaf_count = arrays[0].shape[0]
    shaped = tuple(
        (
            member.reshape((leaf_count // block_size, block_size) + member.shape[1:])
            for member in arrays
        )
    )
    result = lax.map(lambda members: function(*members), shaped)
    return result.reshape((leaf_count,) + result.shape[2:])


def upward(outer, position, charge):
    square = jnp.zeros((position.shape[0], outer.shape[1], position.shape[2]), jnp.float32)
    for dimension in range(3):
        spread = outer[dimension][None, :, None] - position[:, dimension, None, :]
        square = square + spread * spread
    return jnp.einsum("nij,nj->ni", kernel(square), charge, precision=EXACT_DOTS)


def downward(outer, position, weight):
    square = jnp.zeros((position.shape[0], position.shape[2], outer.shape[1]), jnp.float32)
    for dimension in range(3):
        spread = position[:, dimension, :, None] - outer[dimension][None, None, :]
        square = square + spread * spread
    return jnp.einsum("nti,ni->nt", kernel(square), weight, precision=EXACT_DOTS)


def pair_potential(target, source, shift, exclude):
    square = jnp.zeros((target.shape[0], target.shape[2], source.shape[2]), jnp.float32)
    for dimension in range(3):
        spread = target[:, dimension, :, None] - source[:, dimension, None, :] - shift[dimension]
        square = square + spread * spread
    weight = kernel(square)
    if exclude:
        weight = weight * (1.0 - jnp.eye(target.shape[2], dtype=jnp.float32))
    return jnp.einsum("nts,ns->nt", weight, source[:, 3, :], precision=EXACT_DOTS)


def allowed(parity, shift):
    return jnp.abs(jnp.floor_divide(parity + shift, 2)) <= 1


def translate(extended, inner, span_x, span_y, span_z):
    parity_x = jnp.arange(span_x, dtype=jnp.int32) % 2
    parity_y = jnp.arange(span_y, dtype=jnp.int32) % 2
    parity_z = jnp.arange(span_z, dtype=jnp.int32) % 2
    terms_count = inner.shape[1]

    def over_x(accum, shift_x):
        slab = lax.dynamic_slice_in_dim(extended, shift_x + 3, span_x, axis=0)
        okay_x = allowed(parity_x, shift_x)
        spread_x = inner[0][:, None] - inner[0][None, :] - shift_x.astype(jnp.float32)
        pieces = []
        masks = []
        matrices = []
        for shift_y in range(-3, 4):
            rows = slab[:, 3 + shift_y : 3 + shift_y + span_y]
            okay_y = allowed(parity_y, shift_y)
            spread_y = inner[1][:, None] - inner[1][None, :] - float(shift_y)
            for shift_z in range(-3, 4):
                pieces.append(rows[:, :, 3 + shift_z : 3 + shift_z + span_z])
                okay_z = allowed(parity_z, shift_z)
                spread_z = inner[2][:, None] - inner[2][None, :] - float(shift_z)
                matrices.append(
                    kernel(spread_x * spread_x + spread_y * spread_y + spread_z * spread_z)
                )
                extent = jnp.maximum(jnp.maximum(jnp.abs(shift_x), abs(shift_y)), abs(shift_z))
                masks.append(
                    okay_x[:, None, None]
                    & okay_y[None, :, None]
                    & okay_z[None, None, :]
                    & (extent >= 2)
                )
        stacked = jnp.stack(pieces)
        mask = jnp.stack(masks)
        weighted = stacked * mask[..., None].astype(jnp.float32)
        accum = accum + jnp.einsum(
            "oxyzj,oij->xyzi", weighted, jnp.stack(matrices), precision=EXACT_DOTS
        )
        return (accum, None)

    start = jnp.zeros((span_x, span_y, span_z, terms_count), jnp.float32)
    result, _ = lax.scan(over_x, start, jnp.arange(-3, 4, dtype=jnp.int32))
    return result


def axis_bits():
    low_bits = lax.axis_size("gz").bit_length() - 1
    mid_bits = lax.axis_size("gy").bit_length() - 1
    high_bits = lax.axis_size("gx").bit_length() - 1
    return (low_bits, mid_bits, high_bits)


def flip(rising_dens, rising_points, falling_dens, falling_points, global_bit):
    low_bits, mid_bits, high_bits = axis_bits()
    if global_bit < low_bits:
        return from_partner(
            (rising_dens, rising_points, falling_dens, falling_points), "gz", global_bit
        )
    if global_bit < low_bits + mid_bits:
        return from_partner(
            (rising_dens, rising_points, falling_dens, falling_points), "gy", global_bit - low_bits
        )
    return from_partner(
        (rising_dens, rising_points, falling_dens, falling_points),
        "gx",
        global_bit - low_bits - mid_bits,
    )


def box_place(device, dimension, total_bits):
    place = jnp.zeros((), jnp.int32)
    for bit_rank, global_bit in enumerate(range(dimension, total_bits, 3)):
        place = place + jnp.left_shift(
            jnp.bitwise_and(jnp.right_shift(device, global_bit), 1), bit_rank
        )
    return place


def extend(density, points, dimension, layers, device, total_bits):
    position = box_place(device, dimension, total_bits)
    dens_size = density.shape[dimension]
    point_size = points.shape[dimension]
    rising_dens = lax.slice_in_dim(density, dens_size - layers, dens_size, axis=dimension)
    rising_points = lax.slice_in_dim(points, point_size - 1, point_size, axis=dimension)
    falling_dens = lax.slice_in_dim(density, 0, layers, axis=dimension)
    falling_points = lax.slice_in_dim(points, 0, 1, axis=dimension)
    lower_dens = jnp.zeros_like(rising_dens)
    lower_points = jnp.zeros_like(rising_points)
    upper_dens = jnp.zeros_like(falling_dens)
    upper_points = jnp.zeros_like(falling_points)
    carried = (rising_dens, rising_points, falling_dens, falling_points)
    for bit_rank, global_bit in enumerate(range(dimension, total_bits, 3)):
        carried = flip(carried[0], carried[1], carried[2], carried[3], global_bit)
        got_lower = (carried[0], carried[1])
        got_upper = (carried[2], carried[3])
        bit_value = jnp.bitwise_and(jnp.right_shift(position, bit_rank), 1)
        below_bits = jnp.bitwise_and(position, (1 << bit_rank) - 1)
        from_lower = (bit_value == 1) & (below_bits == 0)
        from_upper = (bit_value == 0) & (below_bits == (1 << bit_rank) - 1)
        lower_dens = jnp.where(from_lower, got_lower[0], lower_dens)
        lower_points = jnp.where(from_lower, got_lower[1], lower_points)
        upper_dens = jnp.where(from_upper, got_upper[0], upper_dens)
        upper_points = jnp.where(from_upper, got_upper[1], upper_points)
    density = jnp.concatenate([lower_dens, density, upper_dens], axis=dimension)
    points = jnp.concatenate([lower_points, points, upper_points], axis=dimension)
    return (density, points)


def per_device(positions, charges, counts, up_inverse, down_inverse, inner_surface, outer_surface):
    leaf_total = positions.shape[0]
    block_rows = math.gcd(leaf_total, 64)
    live = (jnp.arange(PTS, dtype=jnp.int32)[None, :] < counts[:, None]).astype(jnp.float32)
    source = charges * live
    check_up = leaf_blocks(partial(upward, outer_surface), (positions, source), block_rows)
    density = jnp.dot(
        check_up, up_inverse.T, preferred_element_type=jnp.float32, precision=EXACT_DOTS
    )
    dens_grid = density.reshape(CX, CY, CZ, TERMS)
    point_grid = jnp.concatenate([positions, source[:, None, :]], axis=1).reshape(
        CX, CY, CZ, 4, PTS
    )
    low_bits, mid_bits, high_bits = axis_bits()
    total_bits = low_bits + mid_bits + high_bits
    device = (lax.axis_index("gx") * lax.axis_size("gy") + lax.axis_index("gy")) * lax.axis_size(
        "gz"
    ) + lax.axis_index("gz")
    layers = 2
    for dimension in range(3):
        dens_grid, point_grid = extend(dens_grid, point_grid, dimension, layers, device, total_bits)
    dens_grid = jnp.pad(dens_grid, ((1, 1), (1, 1), (1, 1), (0, 0)))
    near = jnp.zeros((leaf_total, PTS), jnp.float32)
    for shift_x in range(-1, 2):
        for shift_y in range(-1, 2):
            for shift_z in range(-1, 2):
                window = point_grid[
                    1 + shift_x : 1 + shift_x + CX,
                    1 + shift_y : 1 + shift_y + CY,
                    1 + shift_z : 1 + shift_z + CZ,
                ]
                window = window.reshape(leaf_total, 4, PTS)
                exclude = shift_x == 0 and shift_y == 0 and (shift_z == 0)
                near = near + leaf_blocks(
                    partial(pair_potential, shift=(shift_x, shift_y, shift_z), exclude=exclude),
                    (positions, window),
                    block_rows,
                )
    check_down = translate(dens_grid, inner_surface, CX, CY, CZ).reshape(leaf_total, TERMS)
    local = jnp.dot(
        check_down, down_inverse.T, preferred_element_type=jnp.float32, precision=EXACT_DOTS
    )
    far = leaf_blocks(partial(downward, outer_surface), (positions, local), block_rows)
    return live * (near + far)


def solution(mesh):
    in_specs = (
        P(("gx", "gy", "gz"), None, None),
        P(("gx", "gy", "gz"), None),
        P(("gx", "gy", "gz")),
        P(),
        P(),
        P(),
        P(),
    )
    out_specs = P(("gx", "gy", "gz"), None)
    return jax.shard_map(
        per_device, mesh=mesh, in_specs=in_specs, out_specs=out_specs, check_vma=False
    )
```

profile of v0, /device:TPU:0, one launch (start us, length us, event | category | flops | bytes accessed | tf_op | source)
XLA Modules:
  0.0 531.4 jit_solution(10688036236980636366)
XLA Ops:
  16.4 10.0 %fusion.351 = f32[64,1,128]{2,1,0:T(1,128)} fusion(f32[64,128,1]{1,2,0:T(1,128)S(1)} %bitcast.763, f32[128,128]{1,0:T(8,128)S(1)} %convert_subtract_fusion, f32[64,128]{1,0:T(8,128)S(1)} %get-tuple-element.1106, f32[64,128]{1,0:T(8,128)S(1)} %get-tuple-element.1107, f32[64,128]{1,0:T(8,128)S(1)} %get-tuple-element.1105), kind=kOutput, calls=%fused_computation.617 | convolution fusion | flops 23068672 | bytes 229376 | tf_op jit(solution)/shard_map/while/body/eval_jaxpr/nts,ns->nt/dot_general | solution.py:66
  39.7 10.2 %fusion.235 = f32[64,1,128]{2,1,0:T(1,128)S(1)} fusion(f32[64,128,1]{1,2,0:T(1,128)S(1)} %bitcast.857, f32[64,128]{1,0:T(8,128)S(1)} %get-tuple-element.1083, f32[64,128]{1,0:T(8,128)S(1)} %get-tuple-element.1084, f32[64,128]{1,0:T(8,128)S(1)} %get-tuple-element.1081, f32[64,128]{1,0:T(8,128)S(1)} %get-tuple-element.1106, ...), kind=kOutput, calls=%fused_computation.501 | convolution fusion | flops 23068672 | bytes 262144 | tf_op jit(solution)/shard_map/while/body/eval_jaxpr/nts,ns->nt/dot_general | solution.py:66
  49.9 10.2 %fusion.467 = f32[64,1,128]{2,1,0:T(1,128)S(1)} fusion(f32[64,128,1]{1,2,0:T(1,128)S(1)} %bitcast.858, f32[64,128]{1,0:T(8,128)S(1)} %get-tuple-element.1013, f32[64,128]{1,0:T(8,128)S(1)} %get-tuple-element.1014, f32[64,128]{1,0:T(8,128)S(1)} %get-tuple-element.1011, f32[64,128]{1,0:T(8,128)S(1)} %get-tuple-element.1106, ...), kind=kOutput, calls=%fused_computation.733 | convolution fusion | flops 23068672 | bytes 262144 | tf_op jit(solution)/shard_map/while/body/eval_jaxpr/nts,ns->nt/dot_general | solution.py:66
  60.6 209.7 %while.12 = (s32[]{:T(128)}, f32[4,4,4,64]{3,2,0,1:T(4,128)S(1)}, s32[7]{0:T(128)}, f32[10,10,10,64]{3,2,0,1:T(8,128)S(1)}, f32[3,64]{1,0:T(4,128)S(1)}, /*index...) while((s32[]{:T(128)}, f32[4,4,4,64]{3,2,0,1:T(4,128)S(1)}, ...), condition=%wide.region_1.2_spmd.clone.clone, body=%wide.region_0.1_spmd.clone.clone.sunk | while | flops 156711040 | bytes 9905873 | solution.py:113
  85.7 4.9 fusion.921
  115.6 4.9 fusion.921
  145.5 4.9 fusion.921
  175.4 4.9 fusion.921
  283.0 10.2 %fusion.195 = f32[64,1,128]{2,1,0:T(1,128)S(1)} fusion(f32[64,128,1]{1,2,0:T(1,128)S(1)} %bitcast.852, f32[64,128]{1,0:T(8,128)S(1)} %get-tuple-element.1095, f32[64,128]{1,0:T(8,128)S(1)} %get-tuple-element.1096, f32[64,128]{1,0:T(8,128)S(1)} %get-tuple-element.1093, f32[64,128]{1,0:T(8,128)S(1)} %get-tuple-element.1106, ...), kind=kOutput, calls=%fused_computation.461 | convolution fusion | flops 24117248 | bytes 262144 | tf_op jit(solution)/shard_map/while/body/eval_jaxpr/nts,ns->nt/dot_general | solution.py:66
  293.2 10.2 %fusion.274 = f32[64,1,128]{2,1,0:T(1,128)S(1)} fusion(f32[64,128,1]{1,2,0:T(1,128)S(1)} %bitcast.853, f32[64,128]{1,0:T(8,128)S(1)} %get-tuple-element.1071, f32[64,128]{1,0:T(8,128)S(1)} %get-tuple-element.1072, f32[64,128]{1,0:T(8,128)S(1)} %get-tuple-element.1069, f32[64,128]{1,0:T(8,128)S(1)} %get-tuple-element.1106, ...), kind=kOutput, calls=%fused_computation.540 | convolution fusion | flops 24117248 | bytes 262144 | tf_op jit(solution)/shard_map/while/body/eval_jaxpr/nts,ns->nt/dot_general | solution.py:66
  303.4 10.2 %fusion.314 = f32[64,1,128]{2,1,0:T(1,128)S(1)} fusion(f32[64,128,1]{1,2,0:T(1,128)S(1)} %bitcast.854, f32[64,128]{1,0:T(8,128)S(1)} %get-tuple-element.1059, f32[64,128]{1,0:T(8,128)S(1)} %get-tuple-element.1060, f32[64,128]{1,0:T(8,128)S(1)} %get-tuple-element.1057, f32[64,128]{1,0:T(8,128)S(1)} %get-tuple-element.1106, ...), kind=kOutput, calls=%fused_computation.580 | convolution fusion | flops 23068672 | bytes 262144 | tf_op jit(solution)/shard_map/while/body/eval_jaxpr/nts,ns->nt/dot_general | solution.py:66
  313.7 10.2 %fusion.427 = f32[64,1,128]{2,1,0:T(1,128)S(1)} fusion(f32[64,128,1]{1,2,0:T(1,128)S(1)} %bitcast.855, f32[64,128]{1,0:T(8,128)S(1)} %get-tuple-element.1027, f32[64,128]{1,0:T(8,128)S(1)} %get-tuple-element.1028, f32[64,128]{1,0:T(8,128)S(1)} %get-tuple-element.1025, f32[64,128]{1,0:T(8,128)S(1)} %get-tuple-element.1106, ...), kind=kOutput, calls=%fused_computation.693 | convolution fusion | flops 24117248 | bytes 262144 | tf_op jit(solution)/shard_map/while/body/eval_jaxpr/nts,ns->nt/dot_general | solution.py:66
  323.9 10.2 %fusion.506 = f32[64,1,128]{2,1,0:T(1,128)S(1)} fusion(f32[64,128,1]{1,2,0:T(1,128)S(1)} %bitcast.856, f32[64,128]{1,0:T(8,128)S(1)} %get-tuple-element.997, f32[64,128]{1,0:T(8,128)S(1)} %get-tuple-element.998, f32[64,128]{1,0:T(8,128)S(1)} %get-tuple-element.995, f32[64,128]{1,0:T(8,128)S(1)} %get-tuple-element.1106, ...), kind=kOutput, calls=%fused_computation.772 | convolution fusion | flops 24117248 | bytes 262144 | tf_op jit(solution)/shard_map/while/body/eval_jaxpr/nts,ns->nt/dot_general | solution.py:66
  334.2 10.2 %fusion.388 = f32[64,1,128]{2,1,0:T(1,128)S(1)} fusion(f32[64,128,1]{1,2,0:T(1,128)S(1)} %bitcast.851, f32[64,128]{1,0:T(8,128)S(1)} %get-tuple-element.1039, f32[64,128]{1,0:T(8,128)S(1)} %get-tuple-element.1040, f32[64,128]{1,0:T(8,128)S(1)} %get-tuple-element.1037, f32[64,128]{1,0:T(8,128)S(1)} %get-tuple-element.1106, ...), kind=kOutput, calls=%fused_computation.654 | convolution fusion | flops 23068672 | bytes 262144 | tf_op jit(solution)/shard_map/while/body/eval_jaxpr/nts,ns->nt/dot_general | solution.py:66
  345.6 10.2 %fusion.181 = f32[64,1,128]{2,1,0:T(1,128)S(1)} fusion(f32[64,128,1]{1,2,0:T(1,128)S(1)} %bitcast.834, f32[64,128]{1,0:T(8,128)S(1)} %get-tuple-element.1099, f32[64,128]{1,0:T(8,128)S(1)} %get-tuple-element.1100, f32[64,128]{1,0:T(8,128)S(1)} %get-tuple-element.1097, f32[64,128]{1,0:T(8,128)S(1)} %get-tuple-element.1106, ...), kind=kOutput, calls=%fused_computation.447 | convolution fusion | flops 25165824 | bytes 262144 | tf_op jit(solution)/shard_map/while/body/eval_jaxpr/nts,ns->nt/dot_general | solution.py:66
  355.8 10.2 %fusion.208 = f32[64,1,128]{2,1,0:T(1,128)S(1)} fusion(f32[64,128,1]{1,2,0:T(1,128)S(1)} %bitcast.835, f32[64,128]{1,0:T(8,128)S(1)} %get-tuple-element.1091, f32[64,128]{1,0:T(8,128)S(1)} %get-tuple-element.1092, f32[64,128]{1,0:T(8,128)S(1)} %get-tuple-element.1089, f32[64,128]{1,0:T(8,128)S(1)} %get-tuple-element.1106, ...), kind=kOutput, calls=%fused_computation.474 | convolution fusion | flops 25165824 | bytes 262144 | tf_op jit(solution)/shard_map/while/body/eval_jaxpr/nts,ns->nt/dot_general | solution.py:66
  366.1 10.5 %fusion.222 = f32[64,1,128]{2,1,0:T(1,128)S(1)} fusion(f32[64,128,1]{1,2,0:T(1,128)S(1)} %bitcast.836, f32[64,128]{1,0:T(8,128)S(1)} %get-tuple-element.1087, f32[64,128]{1,0:T(8,128)S(1)} %get-tuple-element.1088, f32[64,128]{1,0:T(8,128)S(1)} %get-tuple-element.1085, f32[64,128]{1,0:T(8,128)S(1)} %get-tuple-element.1106, ...), kind=kOutput, calls=%fused_computation.488 | convolution fusion | flops 24117248 | bytes 262144 | tf_op jit(solution)/shard_map/while/body/eval_jaxpr/nts,ns->nt/dot_general | solution.py:66
  376.6 10.2 %fusion.247 = f32[64,1,128]{2,1,0:T(1,128)S(1)} fusion(f32[64,128,1]{1,2,0:T(1,128)S(1)} %bitcast.837, f32[64,128]{1,0:T(8,128)S(1)} %get-tuple-element.1079, f32[64,128]{1,0:T(8,128)S(1)} %get-tuple-element.1080, f32[64,128]{1,0:T(8,128)S(1)} %get-tuple-element.1077, f32[64,128]{1,0:T(8,128)S(1)} %get-tuple-element.1106, ...), kind=kOutput, calls=%fused_computation.513 | convolution fusion | flops 24117248 | bytes 262144 | tf_op jit(solution)/shard_map/while/body/eval_jaxpr/nts,ns->nt/dot_general | solution.py:66
  386.8 10.3 %fusion.260 = f32[64,1,128]{2,1,0:T(1,128)S(1)} fusion(f32[64,128,1]{1,2,0:T(1,128)S(1)} %bitcast.838, f32[64,128]{1,0:T(8,128)S(1)} %get-tuple-element.1075, f32[64,128]{1,0:T(8,128)S(1)} %get-tuple-element.1076, f32[64,128]{1,0:T(8,128)S(1)} %get-tuple-element.1073, f32[64,128]{1,0:T(8,128)S(1)} %get-tuple-element.1106, ...), kind=kOutput, calls=%fused_computation.526 | convolution fusion | flops 25165824 | bytes 262144 | tf_op jit(solution)/shard_map/while/body/eval_jaxpr/nts,ns->nt/dot_general | solution.py:66
  397.1 10.2 %fusion.287 = f32[64,1,128]{2,1,0:T(1,128)S(1)} fusion(f32[64,128,1]{1,2,0:T(1,128)S(1)} %bitcast.839, f32[64,128]{1,0:T(8,128)S(1)} %get-tuple-element.1067, f32[64,128]{1,0:T(8,128)S(1)} %get-tuple-element.1068, f32[64,128]{1,0:T(8,128)S(1)} %get-tuple-element.1065, f32[64,128]{1,0:T(8,128)S(1)} %get-tuple-element.1106, ...), kind=kOutput, calls=%fused_computation.553 | convolution fusion | flops 25165824 | bytes 262144 | tf_op jit(solution)/shard_map/while/body/eval_jaxpr/nts,ns->nt/dot_general | solution.py:66
  407.3 10.2 %fusion.301 = f32[64,1,128]{2,1,0:T(1,128)S(1)} fusion(f32[64,128,1]{1,2,0:T(1,128)S(1)} %bitcast.840, f32[64,128]{1,0:T(8,128)S(1)} %get-tuple-element.1063, f32[64,128]{1,0:T(8,128)S(1)} %get-tuple-element.1064, f32[64,128]{1,0:T(8,128)S(1)} %get-tuple-element.1061, f32[64,128]{1,0:T(8,128)S(1)} %get-tuple-element.1106, ...), kind=kOutput, calls=%fused_computation.567 | convolution fusion | flops 24117248 | bytes 262144 | tf_op jit(solution)/shard_map/while/body/eval_jaxpr/nts,ns->nt/dot_general | solution.py:66
  417.5 10.2 %fusion.326 = f32[64,1,128]{2,1,0:T(1,128)S(1)} fusion(f32[64,128,1]{1,2,0:T(1,128)S(1)} %bitcast.841, f32[64,128]{1,0:T(8,128)S(1)} %get-tuple-element.1055, f32[64,128]{1,0:T(8,128)S(1)} %get-tuple-element.1056, f32[64,128]{1,0:T(8,128)S(1)} %get-tuple-element.1053, f32[64,128]{1,0:T(8,128)S(1)} %get-tuple-element.1106, ...), kind=kOutput, calls=%fused_computation.592 | convolution fusion | flops 24117248 | bytes 262144 | tf_op jit(solution)/shard_map/while/body/eval_jaxpr/nts,ns->nt/dot_general | solution.py:66
  427.8 10.2 %fusion.339 = f32[64,1,128]{2,1,0:T(1,128)S(1)} fusion(f32[64,128,1]{1,2,0:T(1,128)S(1)} %bitcast.842, f32[64,128]{1,0:T(8,128)S(1)} %get-tuple-element.1051, f32[64,128]{1,0:T(8,128)S(1)} %get-tuple-element.1052, f32[64,128]{1,0:T(8,128)S(1)} %get-tuple-element.1049, f32[64,128]{1,0:T(8,128)S(1)} %get-tuple-element.1106, ...), kind=kOutput, calls=%fused_computation.605 | convolution fusion | flops 23068672 | bytes 262144 | tf_op jit(solution)/shard_map/while/body/eval_jaxpr/nts,ns->nt/dot_general | solution.py:66
  438.0 10.2 %fusion.363 = f32[64,1,128]{2,1,0:T(1,128)S(1)} fusion(f32[64,128,1]{1,2,0:T(1,128)S(1)} %bitcast.843, f32[64,128]{1,0:T(8,128)S(1)} %get-tuple-element.1047, f32[64,128]{1,0:T(8,128)S(1)} %get-tuple-element.1048, f32[64,128]{1,0:T(8,128)S(1)} %get-tuple-element.1045, f32[64,128]{1,0:T(8,128)S(1)} %get-tuple-element.1106, ...), kind=kOutput, calls=%fused_computation.629 | convolution fusion | flops 23068672 | bytes 262144 | tf_op jit(solution)/shard_map/while/body/eval_jaxpr/nts,ns->nt/dot_general | solution.py:66
  448.3 10.2 %fusion.375 = f32[64,1,128]{2,1,0:T(1,128)S(1)} fusion(f32[64,128,1]{1,2,0:T(1,128)S(1)} %bitcast.844, f32[64,128]{1,0:T(8,128)S(1)} %get-tuple-element.1043, f32[64,128]{1,0:T(8,128)S(1)} %get-tuple-element.1044, f32[64,128]{1,0:T(8,128)S(1)} %get-tuple-element.1041, f32[64,128]{1,0:T(8,128)S(1)} %get-tuple-element.1106, ...), kind=kOutput, calls=%fused_computation.641 | convolution fusion | flops 24117248 | bytes 262144 | tf_op jit(solution)/shard_map/while/body/eval_jaxpr/nts,ns->nt/dot_general | solution.py:66
  458.5 10.2 %fusion.400 = f32[64,1,128]{2,1,0:T(1,128)S(1)} fusion(f32[64,128,1]{1,2,0:T(1,128)S(1)} %bitcast.845, f32[64,128]{1,0:T(8,128)S(1)} %get-tuple-element.1035, f32[64,128]{1,0:T(8,128)S(1)} %get-tuple-element.1036, f32[64,128]{1,0:T(8,128)S(1)} %get-tuple-element.1033, f32[64,128]{1,0:T(8,128)S(1)} %get-tuple-element.1106, ...), kind=kOutput, calls=%fused_computation.666 | convolution fusion | flops 24117248 | bytes 262144 | tf_op jit(solution)/shard_map/while/body/eval_jaxpr/nts,ns->nt/dot_general | solution.py:66
  468.8 10.3 %fusion.413 = f32[64,1,128]{2,1,0:T(1,128)S(1)} fusion(f32[64,128,1]{1,2,0:T(1,128)S(1)} %bitcast.846, f32[64,128]{1,0:T(8,128)S(1)} %get-tuple-element.1031, f32[64,128]{1,0:T(8,128)S(1)} %get-tuple-element.1032, f32[64,128]{1,0:T(8,128)S(1)} %get-tuple-element.1029, f32[64,128]{1,0:T(8,128)S(1)} %get-tuple-element.1106, ...), kind=kOutput, calls=%fused_computation.679 | convolution fusion | flops 25165824 | bytes 262144 | tf_op jit(solution)/shard_map/while/body/eval_jaxpr/nts,ns->nt/dot_general | solution.py:66
  479.0 10.2 %fusion.440 = f32[64,1,128]{2,1,0:T(1,128)S(1)} fusion(f32[64,128,1]{1,2,0:T(1,128)S(1)} %bitcast.847, f32[64,128]{1,0:T(8,128)S(1)} %get-tuple-element.1023, f32[64,128]{1,0:T(8,128)S(1)} %get-tuple-element.1024, f32[64,128]{1,0:T(8,128)S(1)} %get-tuple-element.1021, f32[64,128]{1,0:T(8,128)S(1)} %get-tuple-element.1106, ...), kind=kOutput, calls=%fused_computation.706 | convolution fusion | flops 25165824 | bytes 262144 | tf_op jit(solution)/shard_map/while/body/eval_jaxpr/nts,ns->nt/dot_general | solution.py:66
  489.3 10.2 %fusion.454 = f32[64,1,128]{2,1,0:T(1,128)S(1)} fusion(f32[64,128,1]{1,2,0:T(1,128)S(1)} %bitcast.848, f32[64,128]{1,0:T(8,128)S(1)} %get-tuple-element.1019, f32[64,128]{1,0:T(8,128)S(1)} %get-tuple-element.1020, f32[64,128]{1,0:T(8,128)S(1)} %get-tuple-element.1017, f32[64,128]{1,0:T(8,128)S(1)} %get-tuple-element.1106, ...), kind=kOutput, calls=%fused_computation.720 | convolution fusion | flops 24117248 | bytes 262144 | tf_op jit(solution)/shard_map/while/body/eval_jaxpr/nts,ns->nt/dot_general | solution.py:66
  499.5 10.2 %fusion.479 = f32[64,1,128]{2,1,0:T(1,128)S(1)} fusion(f32[64,128,1]{1,2,0:T(1,128)S(1)} %bitcast.849, f32[64,128]{1,0:T(8,128)S(1)} %get-tuple-element.1009, f32[64,128]{1,0:T(8,128)S(1)} %get-tuple-element.1010, f32[64,128]{1,0:T(8,128)S(1)} %get-tuple-element.1007, f32[64,128]{1,0:T(8,128)S(1)} %get-tuple-element.1106, ...), kind=kOutput, calls=%fused_computation.745 | convolution fusion | flops 24117248 | bytes 262144 | tf_op jit(solution)/shard_map/while/body/eval_jaxpr/nts,ns->nt/dot_general | solution.py:66
  509.7 10.3 %fusion.492 = f32[64,1,128]{2,1,0:T(1,128)S(1)} fusion(f32[64,128,1]{1,2,0:T(1,128)S(1)} %bitcast.850, f32[64,128]{1,0:T(8,128)S(1)} %get-tuple-element.1005, f32[64,128]{1,0:T(8,128)S(1)} %get-tuple-element.1006, f32[64,128]{1,0:T(8,128)S(1)} %get-tuple-element.1003, f32[64,128]{1,0:T(8,128)S(1)} %get-tuple-element.1106, ...), kind=kOutput, calls=%fused_computation.758 | convolution fusion | flops 25165824 | bytes 262144 | tf_op jit(solution)/shard_map/while/body/eval_jaxpr/nts,ns->nt/dot_general | solution.py:66
  520.0 10.2 %fusion.519 = f32[64,1,128]{2,1,0:T(1,128)S(1)} fusion(f32[64,128,1]{1,2,0:T(1,128)S(1)} %bitcast.833, f32[64,128]{1,0:T(8,128)S(1)} %get-tuple-element.1001, f32[64,128]{1,0:T(8,128)S(1)} %get-tuple-element.1106, f32[64,128]{1,0:T(8,128)S(1)} %get-tuple-element.1002, f32[64,128]{1,0:T(8,128)S(1)} %get-tuple-element.1107, ...), kind=kOutput, calls=%fused_computation.785 | convolution fusion | flops 25165824 | bytes 262144 | tf_op jit(solution)/shard_map/while/body/eval_jaxpr/nts,ns->nt/dot_general | solution.py:66
  (1285 shorter events, 212.9 us)
Async XLA Ops:
  0.0 6.4 %copy-start = (f32[64,64]{1,0:T(8,128)S(1)}, f32[64,64]{1,0:T(8,128)}, u32[]{:S(2)}) copy-start(f32[64,64]{1,0:T(8,128)} %param.12) | copy-start | bytes 49156
  1.6 4.8 copy-start.9
  1.6 4.8 copy-start.10
  2.4 4.9 copy-start.2
  2.5 4.9 copy-start.7
  2.5 4.9 copy-start.1
  6.7 1.4 collective-permute-start.12
  7.2 3.7 collective-permute-start.10
  7.4 24.5 %collective-permute-start.2 = (f32[1,4,4,4,128]{4,2,1,0,3:T(4,128)S(1)}, f32[1,4,4,4,128]{4,2,1,0,3:T(4,128)S(1)}, u32[]{:S(2)}, u32[]{:S(2)}) collective-permute-start(f32[1,4,4,4,128]{4,2,1,0,3:T(4,128)S(1)} %bitcast.832), channel_id=1, source_target_pairs={{0,1},{1,0},{2,3},{3,2},{4,5},{5,4},{6,7},{7,6},{8,9},{9,8},{10,11... | collective-permute-start | bytes 98312 | tf_op jit(solution)/shard_map/ppermute | solution.py:23
  7.9 24.6 %collective-permute-start = (f32[1,4,4,4,128]{4,2,1,0,3:T(4,128)S(1)}, f32[1,4,4,4,128]{4,2,1,0,3:T(4,128)S(1)}, u32[]{:S(2)}, u32[]{:S(2)}) collective-permute-start(f32[1,4,4,4,128]{4,2,1,0,3:T(4,128)S(1)} %bitcast.831), channel_id=1, source_target_pairs={{0,1},{1,0},{2,3},{3,2},{4,5},{5,4},{6,7},{7,6},{8,9},{9,8},{10,11... | collective-permute-start | bytes 98312 | tf_op jit(solution)/shard_map/ppermute | solution.py:23
  8.1 4.5 collective-permute-start.13
  10.9 3.8 collective-permute-start.11
  14.8 12.1 %collective-permute-start.16 = (f32[8,2,4,64]{3,2,0,1:T(4,128)S(1)}, f32[8,2,4,64]{3,2,0,1:T(4,128)S(1)}, u32[]{:S(2)}, u32[]{:S(2)}) collective-permute-start(f32[8,2,4,64]{3,2,0,1:T(4,128)S(1)} %get-tuple-element.1109), channel_id=1, source_target_pairs={{0,2},{2,0},{4,6},{6,4},{1,3},{3,1},{5,7},{7,5},{8,10},{10,8},{12,... | collective-permute-start | bytes 49160 | tf_op jit(solution)/shard_map/ppermute | solution.py:23
  26.5 3.9 collective-permute-start.14
  26.9 7.0 %collective-permute-start.17 = (f32[8,2,4,64]{3,2,0,1:T(4,128)S(1)}, f32[8,2,4,64]{3,2,0,1:T(4,128)S(1)}, u32[]{:S(2)}, u32[]{:S(2)}) collective-permute-start(f32[8,2,4,64]{3,2,0,1:T(4,128)S(1)} %collective-permute-done.16), channel_id=1, source_target_pairs={{0,16},{8,24},{16,0},{24,8},{1,17},{9,25},{17,1},{25,9},{2,18},{10... | collective-permute-start | bytes 49160 | tf_op jit(solution)/shard_map/ppermute | solution.py:23
  30.4 3.9 collective-permute-start.15
  31.9 5.5 %collective-permute-start.3 = (f32[1,4,4,4,128]{4,2,1,0,3:T(4,128)S(1)}, f32[1,4,4,4,128]{4,2,1,0,3:T(4,128)S(1)}, u32[]{:S(2)}, u32[]{:S(2)}) collective-permute-start(f32[1,4,4,4,128]{4,2,1,0,3:T(4,128)S(1)} %collective-permute-done.2), channel_id=1, source_target_pairs={{0,8},{8,0},{16,24},{24,16},{1,9},{9,1},{17,25},{25,17},{2,10},{10... | collective-permute-start | bytes 98312 | tf_op jit(solution)/shard_map/ppermute | solution.py:23
  32.5 5.0 collective-permute-start.1
  34.4 25.7 %collective-permute-start.19 = (f32[8,8,2,64]{3,2,0,1:T(2,128)S(1)}, f32[8,8,2,64]{3,2,0,1:T(2,128)S(1)}, u32[]{:S(2)}, u32[]{:S(2)}) collective-permute-start(f32[8,8,2,64]{3,2,0,1:T(2,128)S(1)} %get-tuple-element.1104), channel_id=1, source_target_pairs={{0,4},{2,6},{4,0},{6,2},{1,5},{3,7},{5,1},{7,3},{8,12},{10,14},{12... | collective-permute-start | bytes 98312 | tf_op jit(solution)/shard_map/ppermute | solution.py:23
  37.1 23.1 %collective-permute-start.18 = (f32[8,8,2,64]{3,2,0,1:T(2,128)S(1)}, f32[8,8,2,64]{3,2,0,1:T(2,128)S(1)}, u32[]{:S(2)}, u32[]{:S(2)}) collective-permute-start(f32[8,8,2,64]{3,2,0,1:T(2,128)S(1)} %get-tuple-element.1103), channel_id=1, source_target_pairs={{0,4},{2,6},{4,0},{6,2},{1,5},{3,7},{5,1},{7,3},{8,12},{10,14},{12... | collective-permute-start | bytes 98312 | tf_op jit(solution)/shard_map/ppermute | solution.py:23
  37.6 232.9 %collective-permute-start.6 = (f32[6,1,4,4,128]{4,2,1,0,3:T(4,128)S(1)}, f32[6,1,4,4,128]{4,2,1,0,3:T(4,128)S(1)}, u32[]{:S(2)}, u32[]{:S(2)}) collective-permute-start(f32[6,1,4,4,128]{4,2,1,0,3:T(4,128)S(1)} %get-tuple-element.994), channel_id=1, source_target_pairs={{0,2},{2,0},{4,6},{6,4},{1,3},{3,1},{5,7},{7,5},{8,10},{10,8},{12,... | collective-permute-start | bytes 147464 | tf_op jit(solution)/shard_map/ppermute | solution.py:23
  38.1 237.2 %collective-permute-start.4 = (f32[6,1,4,4,128]{4,2,1,0,3:T(4,128)S(1)}, f32[6,1,4,4,128]{4,2,1,0,3:T(4,128)S(1)}, u32[]{:S(2)}, u32[]{:S(2)}) collective-permute-start(f32[6,1,4,4,128]{4,2,1,0,3:T(4,128)S(1)} %get-tuple-element.993), channel_id=1, source_target_pairs={{0,2},{2,0},{4,6},{6,4},{1,3},{3,1},{5,7},{7,5},{8,10},{10,8},{12,... | collective-permute-start | bytes 147464 | tf_op jit(solution)/shard_map/ppermute | solution.py:23
  49.9 10.7 %copy-start.5 = (f32[3,64]{1,0:T(4,128)S(1)}, f32[3,64]{1,0:T(4,128)}, u32[]{:S(2)}) copy-start(f32[3,64]{1,0:T(4,128)} %param.14) | copy-start | bytes 2308
  60.6 209.7 %copy-start.3 = (f32[64,64]{1,0:T(8,128)S(1)}, f32[64,64]{1,0:T(8,128)}, u32[]{:S(2)}) copy-start(f32[64,64]{1,0:T(8,128)} %param.13) | copy-start | bytes 49156
  97.7 1.2 copy-start.6
  187.4 1.2 copy-start.6
  270.5 5.4 %collective-permute-start.7 = (f32[6,1,4,4,128]{4,2,1,0,3:T(4,128)S(1)}, f32[6,1,4,4,128]{4,2,1,0,3:T(4,128)S(1)}, u32[]{:S(2)}, u32[]{:S(2)}) collective-permute-start(f32[6,1,4,4,128]{4,2,1,0,3:T(4,128)S(1)} %collective-permute-done.6), channel_id=1, source_target_pairs={{0,16},{8,24},{16,0},{24,8},{1,17},{9,25},{17,1},{25,9},{2,18},{10... | collective-permute-start | bytes 147464 | tf_op jit(solution)/shard_map/ppermute | solution.py:23
  275.3 4.2 collective-permute-start.5
  279.7 64.7 %collective-permute-start.8 = (f32[6,6,1,4,128]{4,2,1,0,3:T(1,128)S(1)}, f32[6,6,1,4,128]{4,2,1,0,3:T(1,128)S(1)}, u32[]{:S(2)}, u32[]{:S(2)}) collective-permute-start(f32[6,6,1,4,128]{4,2,1,0,3:T(1,128)S(1)} %get-tuple-element.983), channel_id=1, source_target_pairs={{0,4},{2,6},{4,0},{6,2},{1,5},{3,7},{5,1},{7,3},{8,12},{10,14},{12... | collective-permute-start | bytes 221192 | tf_op jit(solution)/shard_map/ppermute | solution.py:23
  282.4 62.1 %collective-permute-start.9 = (f32[6,6,1,4,128]{4,2,1,0,3:T(1,128)S(1)}, f32[6,6,1,4,128]{4,2,1,0,3:T(1,128)S(1)}, u32[]{:S(2)}, u32[]{:S(2)}) collective-permute-start(f32[6,6,1,4,128]{4,2,1,0,3:T(1,128)S(1)} %get-tuple-element.984), channel_id=1, source_target_pairs={{0,4},{2,6},{4,0},{6,2},{1,5},{3,7},{5,1},{7,3},{8,12},{10,14},{12... | collective-permute-start | bytes 221192 | tf_op jit(solution)/shard_map/ppermute | solution.py:23
  520.0 10.3 %copy-start.4 = (f32[64,1,128]{2,1,0:T(1,128)S(1)}, f32[64,1,128]{2,1,0:T(1,128)}, u32[]{:S(2)}) copy-start(f32[64,1,128]{2,1,0:T(1,128)} %fusion.351) | copy-start | bytes 98308
  520.0 10.3 %copy-start.8 = (s32[64]{0:T(128)S(1)}, s32[64]{0:T(128)}, u32[]{:S(2)}) copy-start(s32[64]{0:T(128)} %param.11) | copy-start | bytes 772
  (5 other events, 5.8 us)
where the time goes:
time: 539 us; the launch traced here: 531 us
  matrix products  318 us (59%)
  local copies, waits for them, and re-layouts  114 us (21%)
  other arithmetic  45.9 us (9%)
  starting transfers between devices  21.5 us (4%)
  loops' own time  21.3 us (4%)
  waiting for transfers between devices  9.09 us (2%)
    dot_general x27, matrix products, pair_potential(): jnp.einsum('nts,ns->nt', weight, source[:, 3, :], precision=EXACT_DOTS)  277 us
    and x343, local copies, waits for them, and re-layouts, over_x(): okay_x[:, None, None] & okay_y[None, :, None] & okay_z[None, None, :]  74.2 us
    dot_general x7, matrix products, over_x(): jnp.einsum('oxyzj,oij->xyzi', weighted, jnp.stack(matrices), precision=EX...  34.4 us
    while x336, other arithmetic  33.6 us
    ppermute x20, starting transfers between devices, from_partner(): return lax.ppermute(value, axis, pairs)  21.5 us
    another operation x1, loops' own time, translate(): result, _ = lax.scan(over_x, start, jnp.arange(-3, 4, dtype=jnp.int32))  21.3 us
    while x350, local copies, waits for them, and re-layouts  16.9 us
  transfers between devices with their start and end apart: 20, of which 6 were waited for; matrix products, arithmetic and copies ran while one was open for 52% of the time, Pallas kernels for 0%

commit v1 on v0

v1 whole, which is shorter than its diff:
```python
from functools import partial

import jax
import jax.numpy as jnp
from jax import lax
from jax.experimental import pallas as pl
from jax.experimental.pallas import tpu as pltpu
from jax.sharding import PartitionSpec as P

CX = 4
CY = 4
CZ = 4
PTS = 128
TERMS = 64
LEAF = CX * CY * CZ
EXT = (CX + 2) * (CY + 2) * (CZ + 2)
FEATS = 32


SOFTEN = 0.0025
EXACT_DOTS = lax.Precision.HIGHEST


def from_partner(value, axis, stride):
    mask = 2**stride
    pairs = [(source, source ^ mask) for source in range(lax.axis_size(axis))]
    return lax.ppermute(value, axis, pairs)


def iota(shape, dimension):
    return lax.broadcasted_iota(jnp.int32, shape, dimension)


def column(row):
    size = row.shape[1]
    eye = iota((size, size), 0) == iota((size, size), 1)
    return jnp.sum(jnp.where(eye, row, 0.0), axis=1, keepdims=True)


def rounded(value):
    return value.astype(jnp.bfloat16).astype(jnp.float32)


def three_parts(value):
    high = rounded(value)
    middle = rounded(value - high)
    low = rounded(value - high - middle)
    return high, middle, low


def upward_body(pos_ref, charge_ref, count_ref, up_ref, outer_ref, points_ref, dens_ref):
    lane = iota((1, PTS), 1)
    lanes = iota((TERMS, PTS), 1)
    spots = [jnp.broadcast_to(column(outer_ref[c : c + 1, :]), (TERMS, PTS)) for c in range(3)]

    def leaf(n, check):
        place = pos_ref[n]
        source = jnp.where(lane < count_ref[n], charge_ref[pl.ds(n, 1), :], 0.0)
        points_ref[n] = jnp.concatenate([place, source], axis=0)
        square = jnp.full((TERMS, PTS), SOFTEN, jnp.float32)
        for c in range(3):
            spread = spots[c] - place[c : c + 1, :]
            square = square + spread * spread
        total = jnp.sum(lax.rsqrt(square) * source, axis=1, keepdims=True)
        return jnp.where(lanes == n, total, check)

    check = lax.fori_loop(0, LEAF, leaf, jnp.zeros((TERMS, PTS), jnp.float32), unroll=4)
    dens = jnp.dot(
        up_ref[...], check, preferred_element_type=jnp.float32, precision=EXACT_DOTS
    )
    dens_ref[...] = jnp.transpose(dens)[:LEAF]


def squares_of(points, shift_x, shift_y, shift_z, extra):
    row = iota((8, PTS), 0) % 4
    twice = jnp.concatenate([points, points], axis=0)
    place = twice + jnp.where(row == 0, shift_x, jnp.where(row == 1, shift_y, shift_z))
    square = place * place
    norm = square[0:1] + square[1:2] + square[2:3] + extra
    return jnp.where(row == 3, norm, place), row == 3, iota((8, PTS), 0) < 4


def source_features(points, shift_x, shift_y, shift_z):
    value, last, first = squares_of(points, shift_x, shift_y, shift_z, 0.0)
    high, middle, low = three_parts(value)
    scale = jnp.where(last, 1.0, -2.0)
    high_one = jnp.where(last, 1.0, -2.0 * high)
    middle_one = jnp.where(last, 1.0, -2.0 * middle)
    rows = [
        jnp.where(first, high * scale, middle * scale),
        jnp.where(first, low * scale, high_one),
        jnp.where(first, high_one, middle_one),
        jnp.zeros((8, PTS), jnp.float32),
    ]
    return jnp.concatenate(rows, axis=0).astype(jnp.bfloat16)


def target_features(points, shift_x, shift_y, shift_z):
    value, last, first = squares_of(points, shift_x, shift_y, shift_z, SOFTEN)
    high, middle, low = three_parts(value)
    high_one = jnp.where(last, 1.0, high)
    rows = [
        high_one,
        jnp.where(first, high_one, jnp.where(last, high, middle)),
        jnp.where(first, jnp.where(last, middle, low), jnp.where(last, low, middle)),
        jnp.zeros((8, PTS), jnp.float32),
    ]
    return jnp.transpose(jnp.concatenate(rows, axis=0)).astype(jnp.bfloat16)


def translate_part(dens_ref, inner_ref, down_ref, wide, grouped, local):
    dens = dens_ref[...]
    high = rounded(dens)
    wide[...] = jnp.concatenate([high, rounded(dens - high)], axis=1)

    def clear(n, carry):
        grouped[pl.ds(n * 8, 8)] = jnp.zeros((8, 8, 2 * TERMS), jnp.float32)
        return carry

    lax.fori_loop(0, 64, clear, 0)

    def gather(n, carry):
        a_x = n // 6
        a_y = n % 6
        for a_z in range(6):
            to = (a_x + 1) * 64 + (a_y + 1) * 8 + a_z + 1
            for parent in range(8):
                cell_x = 2 * (parent // 4) + a_x
                cell_y = 2 * (parent // 2 % 2) + a_y
                cell_z = 2 * (parent % 2) + a_z
                cell = cell_x * 64 + cell_y * 8 + cell_z
                grouped[to, parent : parent + 1, :] = wide[pl.ds(cell, 1), :]
        return carry

    lax.fori_loop(0, 36, gather, 0)

    first = iota((TERMS, 2 * TERMS), 1) < TERMS
    spread = []
    for c in range(3):
        row = inner_ref[c : c + 1, :]
        spread.append(jnp.concatenate([row, row], axis=1) - column(row))

    def shift_pair(n, total):
        shift_x = n // 7 - 3
        shift_y = n % 7 - 3
        d_x = spread[0] - shift_x.astype(jnp.float32)
        d_y = spread[1] - shift_y.astype(jnp.float32)
        plane = d_x * d_x + d_y * d_y + SOFTEN
        extent = jnp.maximum(jnp.abs(shift_x), jnp.abs(shift_y))
        lefts = []
        rights = []
        for shift_z in range(-3, 4):
            d_z = spread[2] - float(shift_z)
            weight = lax.rsqrt(plane + d_z * d_z)
            if abs(shift_z) < 2:
                weight = jnp.where(extent >= 2, weight, 0.0)
            upper = rounded(weight)
            right = jnp.where(first, upper, weight - upper).astype(jnp.bfloat16)
            rights += [right, right]
            pieces = []
            for parity in range(8):
                at = (
                    (shift_x + 3 + parity // 4) * 64
                    + (shift_y + 3 + parity // 2 % 2) * 8
                    + shift_z + 3 + parity % 2
                )
                pieces.append(grouped[at])
            lefts.append(jnp.concatenate(pieces, axis=0).astype(jnp.bfloat16))
        for at in range(0, 7, 2):
            left = jnp.concatenate(lefts[at : at + 2], axis=1)
            right = jnp.concatenate(rights[2 * at : 2 * at + 4], axis=0)
            total = total + jnp.dot(left, right, preferred_element_type=jnp.float32)
        return total

    total = lax.fori_loop(0, 49, shift_pair, jnp.zeros((LEAF, 2 * TERMS), jnp.float32))
    down = down_ref[...]
    down = jnp.concatenate([down, down], axis=1)
    down = jnp.concatenate([down, jnp.zeros_like(down)], axis=0)
    local[...] = lax.dot_general(
        total,
        down,
        (((1,), (1,)), ((), ())),
        preferred_element_type=jnp.float32,
        precision=EXACT_DOTS,
    )


def near_body(
    count_ref,
    points_ref,
    dens_ref,
    down_ref,
    inner_ref,
    outer_ref,
    out_ref,
    wide,
    grouped,
    local,
    sources,
    targets,
    surface,
):
    translate_part(dens_ref, inner_ref, down_ref, wide, grouped, local)
    surface[...] = jnp.zeros((4, PTS), jnp.float32)
    surface[0:3, 0:TERMS] = outer_ref[...]

    def middle(cell):
        return cell.astype(jnp.float32) - (CX // 2 + 1)

    def prepare(n, carry):
        e_x = n // ((CY + 2) * (CZ + 2))
        e_y = n // (CZ + 2) % (CY + 2)
        e_z = n % (CZ + 2)
        sources[n] = source_features(points_ref[n], middle(e_x), middle(e_y), middle(e_z))
        return carry

    lax.fori_loop(0, EXT, prepare, 0, unroll=4)

    def ext_index(n):
        return (n // (CY * CZ) + 1) * ((CY + 2) * (CZ + 2)) + (n // CZ % CY + 1) * (CZ + 2) + (
            n % CZ + 1
        )

    def prepare_own(n, carry):
        x = middle(n // (CY * CZ) + 1)
        y = middle(n // CZ % CY + 1)
        z = middle(n % CZ + 1)
        targets[n] = target_features(points_ref[ext_index(n)], x, y, z)
        sources[EXT + n] = source_features(surface[...], x, y, z)
        return carry

    lax.fori_loop(0, LEAF, prepare_own, 0, unroll=4)

    lane = iota((1, PTS), 1)

    def leaf(n, carry):
        base = ext_index(n)
        x = n // (CY * CZ)
        y = n // CZ % CY
        z = n % CZ
        parity = (x % 2) * 4 + (y % 2) * 2 + z % 2
        parent = (x // 2) * 4 + (y // 2) * 2 + z // 2
        count = count_ref[n]
        blocks = []
        for s_x in range(-1, 2):
            for s_y in range(-1, 2):
                for s_z in range(-1, 2):
                    blocks.append(base + s_x * ((CY + 2) * (CZ + 2)) + s_y * (CZ + 2) + s_z)

        def rows(size):
            left = targets[n, 0:size, :]
            eye = iota((size, PTS), 0) == iota((size, PTS), 1)
            total = jnp.zeros((size, PTS), jnp.float32)
            for at in range(0, 28, 2):
                right = []
                charge = []
                for b in (at, at + 1):
                    if b < 27:
                        right.append(sources[blocks[b]])
                        charge.append(points_ref[blocks[b], 3:4, :])
                    else:
                        right.append(sources[EXT + n])
                        charge.append(local[pl.ds(parity * 8 + parent, 1), :])
                square = jnp.dot(
                    left, jnp.concatenate(right, axis=1), preferred_element_type=jnp.float32
                )
                weight = lax.rsqrt(square)
                for k, b in enumerate((at, at + 1)):
                    part = weight[:, k * PTS : (k + 1) * PTS]
                    if b == 13:
                        part = jnp.where(eye, 0.0, part)
                    total = total + part * charge[k]
            sums = jnp.sum(total, axis=1, keepdims=True)
            flat = jnp.sum(jnp.where(eye, sums, 0.0), axis=0, keepdims=True)
            out_ref[pl.ds(n, 1), :] = jnp.where(lane < count, flat, 0.0)

        filled = (count + 31) // 32
        for k in range(1, 5):
            pl.when(filled == k)(partial(rows, 32 * k))
        return carry

    lax.fori_loop(0, LEAF, leaf, 0)


def whole():
    return pl.BlockSpec(memory_space=pltpu.VMEM)


def scalars():
    return pl.BlockSpec(memory_space=pltpu.SMEM)


def upward(positions, charges, counts, up_inverse, outer_surface):
    return pl.pallas_call(
        upward_body,
        out_shape=(
            jax.ShapeDtypeStruct((LEAF, 4, PTS), jnp.float32),
            jax.ShapeDtypeStruct((LEAF, TERMS), jnp.float32),
        ),
        in_specs=[whole(), whole(), scalars(), whole(), whole()],
        out_specs=(whole(), whole()),
        name="upward",
    )(positions, charges, counts, up_inverse, outer_surface)


def potentials(counts, points, density, down_inverse, inner_surface, outer_surface):
    return pl.pallas_call(
        near_body,
        out_shape=jax.ShapeDtypeStruct((LEAF, PTS), jnp.float32),
        in_specs=[scalars()] + [whole()] * 5,
        out_specs=whole(),
        scratch_shapes=[
            pltpu.VMEM((512, 2 * TERMS), jnp.float32),
            pltpu.VMEM((512, 8, 2 * TERMS), jnp.float32),
            pltpu.VMEM((LEAF, 2 * TERMS), jnp.float32),
            pltpu.VMEM((EXT + LEAF, FEATS, PTS), jnp.bfloat16),
            pltpu.VMEM((LEAF, PTS, FEATS), jnp.bfloat16),
            pltpu.VMEM((4, PTS), jnp.float32),
        ],
        compiler_params=pltpu.CompilerParams(vmem_limit_bytes=50 * 2**20),
        name="potentials",
    )(counts, points, density, down_inverse, inner_surface, outer_surface)


def axis_bits():
    low_bits = lax.axis_size("gz").bit_length() - 1
    mid_bits = lax.axis_size("gy").bit_length() - 1
    high_bits = lax.axis_size("gx").bit_length() - 1
    return (low_bits, mid_bits, high_bits)


def flip(rising_dens, rising_points, falling_dens, falling_points, global_bit):
    low_bits, mid_bits, high_bits = axis_bits()
    if global_bit < low_bits:
        return from_partner(
            (rising_dens, rising_points, falling_dens, falling_points), "gz", global_bit
        )
    if global_bit < low_bits + mid_bits:
        return from_partner(
            (rising_dens, rising_points, falling_dens, falling_points), "gy", global_bit - low_bits
        )
    return from_partner(
        (rising_dens, rising_points, falling_dens, falling_points),
        "gx",
        global_bit - low_bits - mid_bits,
    )


def box_place(device, dimension, total_bits):
    place = jnp.zeros((), jnp.int32)
    for bit_rank, global_bit in enumerate(range(dimension, total_bits, 3)):
        place = place + jnp.left_shift(
            jnp.bitwise_and(jnp.right_shift(device, global_bit), 1), bit_rank
        )
    return place


def extend(density, points, dimension, layers, device, total_bits):
    position = box_place(device, dimension, total_bits)
    dens_size = density.shape[dimension]
    point_size = points.shape[dimension]
    rising_dens = lax.slice_in_dim(density, dens_size - layers, dens_size, axis=dimension)
    rising_points = lax.slice_in_dim(points, point_size - 1, point_size, axis=dimension)
    falling_dens = lax.slice_in_dim(density, 0, layers, axis=dimension)
    falling_points = lax.slice_in_dim(points, 0, 1, axis=dimension)
    lower_dens = jnp.zeros_like(rising_dens)
    lower_points = jnp.zeros_like(rising_points)
    upper_dens = jnp.zeros_like(falling_dens)
    upper_points = jnp.zeros_like(falling_points)
    carried = (rising_dens, rising_points, falling_dens, falling_points)
    for bit_rank, global_bit in enumerate(range(dimension, total_bits, 3)):
        carried = flip(carried[0], carried[1], carried[2], carried[3], global_bit)
        got_lower = (carried[0], carried[1])
        got_upper = (carried[2], carried[3])
        bit_value = jnp.bitwise_and(jnp.right_shift(position, bit_rank), 1)
        below_bits = jnp.bitwise_and(position, (1 << bit_rank) - 1)
        from_lower = (bit_value == 1) & (below_bits == 0)
        from_upper = (bit_value == 0) & (below_bits == (1 << bit_rank) - 1)
        lower_dens = jnp.where(from_lower, got_lower[0], lower_dens)
        lower_points = jnp.where(from_lower, got_lower[1], lower_points)
        upper_dens = jnp.where(from_upper, got_upper[0], upper_dens)
        upper_points = jnp.where(from_upper, got_upper[1], upper_points)
    density = jnp.concatenate([lower_dens, density, upper_dens], axis=dimension)
    points = jnp.concatenate([lower_points, points, upper_points], axis=dimension)
    return (density, points)


def per_device(positions, charges, counts, up_inverse, down_inverse, inner_surface, outer_surface):
    point_flat, density = upward(positions, charges, counts, up_inverse, outer_surface)
    dens_grid = density.reshape(CX, CY, CZ, TERMS)
    point_grid = point_flat.reshape(CX, CY, CZ, 4, PTS)
    low_bits, mid_bits, high_bits = axis_bits()
    total_bits = low_bits + mid_bits + high_bits
    device = (lax.axis_index("gx") * lax.axis_size("gy") + lax.axis_index("gy")) * lax.axis_size(
        "gz"
    ) + lax.axis_index("gz")
    for dimension in range(3):
        dens_grid, point_grid = extend(dens_grid, point_grid, dimension, 2, device, total_bits)
    return potentials(
        counts,
        point_grid.reshape(EXT, 4, PTS),
        dens_grid.reshape(512, TERMS),
        down_inverse,
        inner_surface,
        outer_surface,
    )


def solution(mesh):
    in_specs = (
        P(("gx", "gy", "gz"), None, None),
        P(("gx", "gy", "gz"), None),
        P(("gx", "gy", "gz")),
        P(),
        P(),
        P(),
        P(),
    )
    out_specs = P(("gx", "gy", "gz"), None)
    return jax.shard_map(
        per_device, mesh=mesh, in_specs=in_specs, out_specs=out_specs, check_vma=False
    )
```

time: 539 us -> 99 us (0.18); the launches traced: 531 us -> 98.8 us
  matrix products: 318 us -> 0 us
  local copies, waits for them, and re-layouts: 114 us -> 3.88 us
  Pallas kernels: 0 us -> 52.8 us
  other arithmetic: 45.9 us -> 0.53 us
  loops' own time: 21.3 us -> 0 us
  waiting for transfers between devices: 9.09 us -> 21.5 us
    dot_general x38 -> x0, matrix products: 318 us -> none  [the longest x27 277 us: pair_potential(): jnp.einsum('nts,ns->nt', weight, source[:, 3, :], precision=EXACT_DOTS)]
    and x343 -> x0, local copies, waits for them, and re-layouts: 74.2 us -> none  [over_x(): okay_x[:, None, None] & okay_y[None, :, None] & okay_z[None, None, :]]
    pallas_call x0 -> x2, Pallas kernels: none -> 52.8 us  [the longest x1 48.8 us: potentials(): pl.pallas_call(near_body, out_shape=jax.ShapeDtypeStruct((LEAF, PTS), jnp...]
    while x336 -> x0, other arithmetic: 33.6 us -> none
    another operation x1 -> x0, loops' own time: 21.3 us -> none  [translate(): result, _ = lax.scan(over_x, start, jnp.arange(-3, 4, dtype=jnp.int32))]
    while x351 -> x0, local copies, waits for them, and re-layouts: 16.9 us -> none
    ppermute x20, waiting for transfers between devices: 9.09 us -> 21.5 us  [from_partner(): return lax.ppermute(value, axis, pairs)]
    another operation x14 -> x0, local copies, waits for them, and re-layouts: 9.85 us -> none  [the longest x7 9.65 us: over_x(): mask = jnp.stack(masks)]
  transfers between devices with their start and end apart: 20 -> 20, of which waited for: 6 -> 11; matrix products, arithmetic and copies ran while one was open for 52% -> 1% of each run, Pallas kernels for 0% -> 0%
where the time goes in v1:
time: 99 us; the launch traced here: 98.8 us
  Pallas kernels  52.8 us (53%)
  waiting for transfers between devices  21.5 us (22%)
  starting transfers between devices  19.9 us (20%)
  local copies, waits for them, and re-layouts  3.88 us (4%)
    pallas_call x1, Pallas kernels, potentials(): pl.pallas_call(near_body, out_shape=jax.ShapeDtypeStruct((LEAF, PTS), jnp...  48.8 us
    ppermute x20, waiting for transfers between devices, from_partner(): return lax.ppermute(value, axis, pairs)  21.5 us
    ppermute x20, starting transfers between devices, from_partner(): return lax.ppermute(value, axis, pairs)  19.9 us
    pallas_call x1, Pallas kernels, upward(): pl.pallas_call(upward_body, out_shape=(jax.ShapeDtypeStruct((LEAF, 4, PTS...  4.05 us
    unnamed x13, local copies, waits for them, and re-layouts  2.3 us
  transfers between devices with their start and end apart: 20, of which 11 were waited for; matrix products, arithmetic and copies ran while one was open for 1% of the time, Pallas kernels for 0%

profile of v1, /device:TPU:0, one launch (start us, length us, event | category | flops | bytes accessed | tf_op | source)
XLA Modules:
  0.0 98.8 jit_solution(11278581674049674375)
XLA Ops:
  0.0 1.6 %copy.8.pos_ref = f32[64,3,128]{2,1,0:T(4,128)} copy(f32[64,3,128]{2,0,1:T(8,128)} %param.7) | data formatting | bytes 196608 | tf_op args[0]
  1.6 4.1 %upward.1 = (f32[64,4,128]{2,1,0:T(4,128)}, f32[64,64]{1,0:T(8,128)}) custom-call(f32[64,3,128]{2,1,0:T(4,128)} %copy.8.pos_ref, f32[64,128]{1,0:T(8,128)} %charge_ref.1, s32[64]{0:T(128)} %count_ref.3, f32[64,64]{1,0:T(8,128)} %up_ref.1, f32[3,64]{1,0:T(4,128)} %outer_ref.3), custom_call_target="tpu_custom_call" | custom-call | tf_op jit(solution)/shard_map/upward/pallas_call | solution.py:294
  5.7 0.7 fusion.3
  6.4 0.5 collective-permute-start.12
  6.9 0.8 collective-permute-done.12
  7.7 2.8 %collective-permute-start.13 = (f32[2,4,4,64]{3,2,1,0:T(4,128)S(1)}, f32[2,4,4,64]{3,2,1,0:T(4,128)S(1)}, u32[]{:S(2)}, u32[]{:S(2)}) collective-permute-start(f32[2,4,4,64]{3,2,1,0:T(4,128)S(1)} %collective-permute-done.12), channel_id=1, source_target_pairs={{0,8},{8,0},{16,24},{24,16},{1,9},{9,1},{17,25},{25,17},{2,10},{10... | collective-permute-start | bytes 24584 | tf_op jit(solution)/shard_map/ppermute | solution.py:27
  10.6 0.8 fusion.1
  11.3 0.5 collective-permute-start
  11.9 0.4 collective-permute-done.13
  12.3 3.3 %collective-permute-done.11 = f32[2,4,4,64]{3,2,1,0:T(4,128)S(1)} collective-permute-done((f32[2,4,4,64]{3,2,1,0:T(4,128)S(1)}, f32[2,4,4,64]{3,2,1,0:T(4,128)S(1)}, u32[]{:S(2)}, u32[]{:S(2)}) %collective-permute-start.11) | collective-permute-done | bytes 8224 | tf_op jit(solution)/shard_map/ppermute | solution.py:27
  15.7 1.6 %collective-permute-start.16 = (f32[8,2,4,64]{3,2,1,0:T(4,128)S(1)}, f32[8,2,4,64]{3,2,1,0:T(4,128)S(1)}, u32[]{:S(2)}, u32[]{:S(2)}) collective-permute-start(f32[8,2,4,64]{3,2,1,0:T(4,128)S(1)} %get-tuple-element.18), channel_id=1, source_target_pairs={{0,2},{2,0},{4,6},{6,4},{1,3},{3,1},{5,7},{7,5},{8,10},{10,8},{12,... | collective-permute-start | bytes 49160 | tf_op jit(solution)/shard_map/ppermute | solution.py:27
  17.3 0.4 collective-permute-start.14
  17.7 1.9 %collective-permute-done.16 = f32[8,2,4,64]{3,2,1,0:T(4,128)S(1)} collective-permute-done((f32[8,2,4,64]{3,2,1,0:T(4,128)S(1)}, f32[8,2,4,64]{3,2,1,0:T(4,128)S(1)}, u32[]{:S(2)}, u32[]{:S(2)}) %collective-permute-start.16) | collective-permute-done | bytes 16416 | tf_op jit(solution)/shard_map/ppermute | solution.py:27
  19.6 1.5 %collective-permute-start.17 = (f32[8,2,4,64]{3,2,1,0:T(4,128)S(1)}, f32[8,2,4,64]{3,2,1,0:T(4,128)S(1)}, u32[]{:S(2)}, u32[]{:S(2)}) collective-permute-start(f32[8,2,4,64]{3,2,1,0:T(4,128)S(1)} %collective-permute-done.16), channel_id=1, source_target_pairs={{0,16},{8,24},{16,0},{24,8},{1,17},{9,25},{17,1},{25,9},{2,18},{10... | collective-permute-start | bytes 49160 | tf_op jit(solution)/shard_map/ppermute | solution.py:27
  21.2 0.5 collective-permute-start.3
  21.7 1.5 %collective-permute-start.1 = (f32[1,4,4,4,128]{4,3,2,1,0:T(4,128)S(1)}, f32[1,4,4,4,128]{4,3,2,1,0:T(4,128)S(1)}, u32[]{:S(2)}, u32[]{:S(2)}) collective-permute-start(f32[1,4,4,4,128]{4,3,2,1,0:T(4,128)S(1)} %collective-permute-done), channel_id=1, source_target_pairs={{0,8},{8,0},{16,24},{24,16},{1,9},{9,1},{17,25},{25,17},{2,10},{10... | collective-permute-start | bytes 98312 | tf_op jit(solution)/shard_map/ppermute | solution.py:27
  23.2 0.5 collective-permute-start.15
  23.7 3.4 %collective-permute-done.15 = f32[8,2,4,64]{3,2,1,0:T(4,128)S(1)} collective-permute-done((f32[8,2,4,64]{3,2,1,0:T(4,128)S(1)}, f32[8,2,4,64]{3,2,1,0:T(4,128)S(1)}, u32[]{:S(2)}, u32[]{:S(2)}) %collective-permute-start.15) | collective-permute-done | bytes 16416 | tf_op jit(solution)/shard_map/ppermute | solution.py:27
  27.2 2.7 %collective-permute-start.19 = (f32[8,8,2,64]{3,2,1,0:T(2,128)S(1)}, f32[8,8,2,64]{3,2,1,0:T(2,128)S(1)}, u32[]{:S(2)}, u32[]{:S(2)}) collective-permute-start(f32[8,8,2,64]{3,2,1,0:T(2,128)S(1)} %get-tuple-element.14), channel_id=1, source_target_pairs={{0,4},{2,6},{4,0},{6,2},{1,5},{3,7},{5,1},{7,3},{8,12},{10,14},{12... | collective-permute-start | bytes 98312 | tf_op jit(solution)/shard_map/ppermute | solution.py:27
  29.9 0.3 collective-permute-start.18
  30.3 1.6 %collective-permute-start.6 = (f32[6,1,4,4,128]{4,3,2,1,0:T(4,128)S(1)}, f32[6,1,4,4,128]{4,3,2,1,0:T(4,128)S(1)}, u32[]{:S(2)}, u32[]{:S(2)}) collective-permute-start(f32[6,1,4,4,128]{4,3,2,1,0:T(4,128)S(1)} %get-tuple-element.12), channel_id=1, source_target_pairs={{0,2},{2,0},{4,6},{6,4},{1,3},{3,1},{5,7},{7,5},{8,10},{10,8},{12,... | collective-permute-start | bytes 147464 | tf_op jit(solution)/shard_map/ppermute | solution.py:27
  32.0 0.4 collective-permute-start.4
  32.5 2.7 %collective-permute-done.6 = f32[6,1,4,4,128]{4,3,2,1,0:T(4,128)S(1)} collective-permute-done((f32[6,1,4,4,128]{4,3,2,1,0:T(4,128)S(1)}, f32[6,1,4,4,128]{4,3,2,1,0:T(4,128)S(1)}, u32[]{:S(2)}, u32[]{:S(2)}) %collective-permute-start.6) | collective-permute-done | bytes 49184 | tf_op jit(solution)/shard_map/ppermute | solution.py:27
  35.2 0.5 collective-permute-start.7
  36.1 1.3 %collective-permute-start.5 = (f32[6,1,4,4,128]{4,3,2,1,0:T(4,128)S(1)}, f32[6,1,4,4,128]{4,3,2,1,0:T(4,128)S(1)}, u32[]{:S(2)}, u32[]{:S(2)}) collective-permute-start(f32[6,1,4,4,128]{4,3,2,1,0:T(4,128)S(1)} %collective-permute-done.4), channel_id=1, source_target_pairs={{0,16},{8,24},{16,0},{24,8},{1,17},{9,25},{17,1},{25,9},{2,18},{10... | collective-permute-start | bytes 147464 | tf_op jit(solution)/shard_map/ppermute | solution.py:27
  37.3 2.0 %collective-permute-done.7 = f32[6,1,4,4,128]{4,3,2,1,0:T(4,128)S(1)} collective-permute-done((f32[6,1,4,4,128]{4,3,2,1,0:T(4,128)S(1)}, f32[6,1,4,4,128]{4,3,2,1,0:T(4,128)S(1)}, u32[]{:S(2)}, u32[]{:S(2)}) %collective-permute-start.7) | collective-permute-done | bytes 49184 | tf_op jit(solution)/shard_map/ppermute | solution.py:27
  39.3 0.9 collective-permute-done.5
  40.2 2.8 %collective-permute-start.9 = (f32[6,6,1,4,128]{4,3,2,1,0:T(4,128)S(1)}, f32[6,6,1,4,128]{4,3,2,1,0:T(4,128)S(1)}, u32[]{:S(2)}, u32[]{:S(2)}) collective-permute-start(f32[6,6,1,4,128]{4,3,2,1,0:T(4,128)S(1)} %get-tuple-element.10), channel_id=1, source_target_pairs={{0,4},{2,6},{4,0},{6,2},{1,5},{3,7},{5,1},{7,3},{8,12},{10,14},{12... | collective-permute-start | bytes 221192 | tf_op jit(solution)/shard_map/ppermute | solution.py:27
  43.4 2.9 %collective-permute-done.9 = f32[6,6,1,4,128]{4,3,2,1,0:T(4,128)S(1)} collective-permute-done((f32[6,6,1,4,128]{4,3,2,1,0:T(4,128)S(1)}, f32[6,6,1,4,128]{4,3,2,1,0:T(4,128)S(1)}, u32[]{:S(2)}, u32[]{:S(2)}) %collective-permute-start.9) | collective-permute-done | bytes 73760 | tf_op jit(solution)/shard_map/ppermute | solution.py:27
  46.3 2.9 %collective-permute-done.8 = f32[6,6,1,4,128]{4,3,2,1,0:T(4,128)S(1)} collective-permute-done((f32[6,6,1,4,128]{4,3,2,1,0:T(4,128)S(1)}, f32[6,6,1,4,128]{4,3,2,1,0:T(4,128)S(1)}, u32[]{:S(2)}, u32[]{:S(2)}) %collective-permute-start.8) | collective-permute-done | bytes 73760 | tf_op jit(solution)/shard_map/ppermute | solution.py:27
  49.4 0.6 copy-done
  50.0 48.8 %potentials.1 = f32[64,128]{1,0:T(8,128)} custom-call(s32[64]{0:T(128)S(1)} %copy-done.3, f32[216,4,128]{2,1,0:T(4,128)S(1)} %bitcast.8, f32[512,64]{1,0:T(8,128)S(1)} %bitcast.9, f32[64,64]{1,0:T(8,128)S(1)} %copy-done, f32[3,64]{1,0:T(4,128)S(1)} %copy-done.2, f32[3,64]{1,0:T(4,128)S(1)} %copy-done.1), custom_call_target="tpu_custom_call" | custom-call | tf_op jit(solution)/shard_map/potentials/pallas_call | solution.py:307
  (45 shorter events, 1.4 us)
Async XLA Ops:
  6.4 1.3 %collective-permute-start.12 = (f32[2,4,4,64]{3,2,1,0:T(4,128)S(1)}, f32[2,4,4,64]{3,2,1,0:T(4,128)S(1)}, u32[]{:S(2)}, u32[]{:S(2)}) collective-permute-start(f32[2,4,4,64]{3,2,1,0:T(4,128)S(1)} %bitcast.19), channel_id=1, source_target_pairs={{0,1},{1,0},{2,3},{3,2},{4,5},{5,4},{6,7},{7,6},{8,9},{9,8},{10,11... | collective-permute-start | bytes 24584 | tf_op jit(solution)/shard_map/ppermute | solution.py:27
  6.9 5.0 %collective-permute-start.10 = (f32[2,4,4,64]{3,2,1,0:T(4,128)S(1)}, f32[2,4,4,64]{3,2,1,0:T(4,128)S(1)}, u32[]{:S(2)}, u32[]{:S(2)}) collective-permute-start(f32[2,4,4,64]{3,2,1,0:T(4,128)S(1)} %bitcast.18), channel_id=1, source_target_pairs={{0,1},{1,0},{2,3},{3,2},{4,5},{5,4},{6,7},{7,6},{8,9},{9,8},{10,11... | collective-permute-start | bytes 24584 | tf_op jit(solution)/shard_map/ppermute | solution.py:27
  7.7 4.5 %collective-permute-start.13 = (f32[2,4,4,64]{3,2,1,0:T(4,128)S(1)}, f32[2,4,4,64]{3,2,1,0:T(4,128)S(1)}, u32[]{:S(2)}, u32[]{:S(2)}) collective-permute-start(f32[2,4,4,64]{3,2,1,0:T(4,128)S(1)} %collective-permute-done.12), channel_id=1, source_target_pairs={{0,8},{8,0},{16,24},{24,16},{1,9},{9,1},{17,25},{25,17},{2,10},{10... | collective-permute-start | bytes 24584 | tf_op jit(solution)/shard_map/ppermute | solution.py:27
  11.3 9.8 %collective-permute-start.2 = (f32[1,4,4,4,128]{4,3,2,1,0:T(4,128)S(1)}, f32[1,4,4,4,128]{4,3,2,1,0:T(4,128)S(1)}, u32[]{:S(2)}, u32[]{:S(2)}) collective-permute-start(f32[1,4,4,4,128]{4,3,2,1,0:T(4,128)S(1)} %bitcast.17), channel_id=1, source_target_pairs={{0,1},{1,0},{2,3},{3,2},{4,5},{5,4},{6,7},{7,6},{8,9},{9,8},{10,11... | collective-permute-start | bytes 98312 | tf_op jit(solution)/shard_map/ppermute | solution.py:27
  11.3 10.3 %collective-permute-start = (f32[1,4,4,4,128]{4,3,2,1,0:T(4,128)S(1)}, f32[1,4,4,4,128]{4,3,2,1,0:T(4,128)S(1)}, u32[]{:S(2)}, u32[]{:S(2)}) collective-permute-start(f32[1,4,4,4,128]{4,3,2,1,0:T(4,128)S(1)} %bitcast.16), channel_id=1, source_target_pairs={{0,1},{1,0},{2,3},{3,2},{4,5},{5,4},{6,7},{7,6},{8,9},{9,8},{10,11... | collective-permute-start | bytes 98312 | tf_op jit(solution)/shard_map/ppermute | solution.py:27
  11.9 3.7 %collective-permute-start.11 = (f32[2,4,4,64]{3,2,1,0:T(4,128)S(1)}, f32[2,4,4,64]{3,2,1,0:T(4,128)S(1)}, u32[]{:S(2)}, u32[]{:S(2)}) collective-permute-start(f32[2,4,4,64]{3,2,1,0:T(4,128)S(1)} %collective-permute-done.10), channel_id=1, source_target_pairs={{0,8},{8,0},{16,24},{24,16},{1,9},{9,1},{17,25},{25,17},{2,10},{10... | collective-permute-start | bytes 24584 | tf_op jit(solution)/shard_map/ppermute | solution.py:27
  12.3 3.3 %copy-start.5 = (f32[64,64]{1,0:T(8,128)S(1)}, f32[64,64]{1,0:T(8,128)}, u32[]{:S(2)}) copy-start(f32[64,64]{1,0:T(8,128)} %get-tuple-element.8) | copy-start | bytes 49156
  15.7 4.0 %collective-permute-start.16 = (f32[8,2,4,64]{3,2,1,0:T(4,128)S(1)}, f32[8,2,4,64]{3,2,1,0:T(4,128)S(1)}, u32[]{:S(2)}, u32[]{:S(2)}) collective-permute-start(f32[8,2,4,64]{3,2,1,0:T(4,128)S(1)} %get-tuple-element.18), channel_id=1, source_target_pairs={{0,2},{2,0},{4,6},{6,4},{1,3},{3,1},{5,7},{7,5},{8,10},{10,8},{12,... | collective-permute-start | bytes 49160 | tf_op jit(solution)/shard_map/ppermute | solution.py:27
  17.3 5.9 %collective-permute-start.14 = (f32[8,2,4,64]{3,2,1,0:T(4,128)S(1)}, f32[8,2,4,64]{3,2,1,0:T(4,128)S(1)}, u32[]{:S(2)}, u32[]{:S(2)}) collective-permute-start(f32[8,2,4,64]{3,2,1,0:T(4,128)S(1)} %get-tuple-element.17), channel_id=1, source_target_pairs={{0,2},{2,0},{4,6},{6,4},{1,3},{3,1},{5,7},{7,5},{8,10},{10,8},{12,... | collective-permute-start | bytes 49160 | tf_op jit(solution)/shard_map/ppermute | solution.py:27
  19.6 4.1 %collective-permute-start.17 = (f32[8,2,4,64]{3,2,1,0:T(4,128)S(1)}, f32[8,2,4,64]{3,2,1,0:T(4,128)S(1)}, u32[]{:S(2)}, u32[]{:S(2)}) collective-permute-start(f32[8,2,4,64]{3,2,1,0:T(4,128)S(1)} %collective-permute-done.16), channel_id=1, source_target_pairs={{0,16},{8,24},{16,0},{24,8},{1,17},{9,25},{17,1},{25,9},{2,18},{10... | collective-permute-start | bytes 49160 | tf_op jit(solution)/shard_map/ppermute | solution.py:27
  21.2 9.1 %collective-permute-start.3 = (f32[1,4,4,4,128]{4,3,2,1,0:T(4,128)S(1)}, f32[1,4,4,4,128]{4,3,2,1,0:T(4,128)S(1)}, u32[]{:S(2)}, u32[]{:S(2)}) collective-permute-start(f32[1,4,4,4,128]{4,3,2,1,0:T(4,128)S(1)} %collective-permute-done.2), channel_id=1, source_target_pairs={{0,8},{8,0},{16,24},{24,16},{1,9},{9,1},{17,25},{25,17},{2,10},{10... | collective-permute-start | bytes 98312 | tf_op jit(solution)/shard_map/ppermute | solution.py:27
  21.7 8.6 %collective-permute-start.1 = (f32[1,4,4,4,128]{4,3,2,1,0:T(4,128)S(1)}, f32[1,4,4,4,128]{4,3,2,1,0:T(4,128)S(1)}, u32[]{:S(2)}, u32[]{:S(2)}) collective-permute-start(f32[1,4,4,4,128]{4,3,2,1,0:T(4,128)S(1)} %collective-permute-done), channel_id=1, source_target_pairs={{0,8},{8,0},{16,24},{24,16},{1,9},{9,1},{17,25},{25,17},{2,10},{10... | collective-permute-start | bytes 98312 | tf_op jit(solution)/shard_map/ppermute | solution.py:27
  23.2 3.9 %collective-permute-start.15 = (f32[8,2,4,64]{3,2,1,0:T(4,128)S(1)}, f32[8,2,4,64]{3,2,1,0:T(4,128)S(1)}, u32[]{:S(2)}, u32[]{:S(2)}) collective-permute-start(f32[8,2,4,64]{3,2,1,0:T(4,128)S(1)} %collective-permute-done.14), channel_id=1, source_target_pairs={{0,16},{8,24},{16,0},{24,8},{1,17},{9,25},{17,1},{25,9},{2,18},{10... | collective-permute-start | bytes 49160 | tf_op jit(solution)/shard_map/ppermute | solution.py:27
  27.2 3.1 %copy-start.4 = (f32[64,4,128]{2,1,0:T(4,128)S(1)}, f32[64,4,128]{2,1,0:T(4,128)}, u32[]{:S(2)}) copy-start(f32[64,4,128]{2,1,0:T(4,128)} %get-tuple-element.7) | copy-start | bytes 393220
  27.2 5.2 %collective-permute-start.19 = (f32[8,8,2,64]{3,2,1,0:T(2,128)S(1)}, f32[8,8,2,64]{3,2,1,0:T(2,128)S(1)}, u32[]{:S(2)}, u32[]{:S(2)}) collective-permute-start(f32[8,8,2,64]{3,2,1,0:T(2,128)S(1)} %get-tuple-element.14), channel_id=1, source_target_pairs={{0,4},{2,6},{4,0},{6,2},{1,5},{3,7},{5,1},{7,3},{8,12},{10,14},{12... | collective-permute-start | bytes 98312 | tf_op jit(solution)/shard_map/ppermute | solution.py:27
  29.9 5.8 %collective-permute-start.18 = (f32[8,8,2,64]{3,2,1,0:T(2,128)S(1)}, f32[8,8,2,64]{3,2,1,0:T(2,128)S(1)}, u32[]{:S(2)}, u32[]{:S(2)}) collective-permute-start(f32[8,8,2,64]{3,2,1,0:T(2,128)S(1)} %get-tuple-element.13), channel_id=1, source_target_pairs={{0,4},{2,6},{4,0},{6,2},{1,5},{3,7},{5,1},{7,3},{8,12},{10,14},{12... | collective-permute-start | bytes 98312 | tf_op jit(solution)/shard_map/ppermute | solution.py:27
  30.3 4.9 %collective-permute-start.6 = (f32[6,1,4,4,128]{4,3,2,1,0:T(4,128)S(1)}, f32[6,1,4,4,128]{4,3,2,1,0:T(4,128)S(1)}, u32[]{:S(2)}, u32[]{:S(2)}) collective-permute-start(f32[6,1,4,4,128]{4,3,2,1,0:T(4,128)S(1)} %get-tuple-element.12), channel_id=1, source_target_pairs={{0,2},{2,0},{4,6},{6,4},{1,3},{3,1},{5,7},{7,5},{8,10},{10,8},{12,... | collective-permute-start | bytes 147464 | tf_op jit(solution)/shard_map/ppermute | solution.py:27
  32.0 4.1 %collective-permute-start.4 = (f32[6,1,4,4,128]{4,3,2,1,0:T(4,128)S(1)}, f32[6,1,4,4,128]{4,3,2,1,0:T(4,128)S(1)}, u32[]{:S(2)}, u32[]{:S(2)}) collective-permute-start(f32[6,1,4,4,128]{4,3,2,1,0:T(4,128)S(1)} %get-tuple-element.11), channel_id=1, source_target_pairs={{0,2},{2,0},{4,6},{6,4},{1,3},{3,1},{5,7},{7,5},{8,10},{10,8},{12,... | collective-permute-start | bytes 147464 | tf_op jit(solution)/shard_map/ppermute | solution.py:27
  35.2 4.1 %collective-permute-start.7 = (f32[6,1,4,4,128]{4,3,2,1,0:T(4,128)S(1)}, f32[6,1,4,4,128]{4,3,2,1,0:T(4,128)S(1)}, u32[]{:S(2)}, u32[]{:S(2)}) collective-permute-start(f32[6,1,4,4,128]{4,3,2,1,0:T(4,128)S(1)} %collective-permute-done.6), channel_id=1, source_target_pairs={{0,16},{8,24},{16,0},{24,8},{1,17},{9,25},{17,1},{25,9},{2,18},{10... | collective-permute-start | bytes 147464 | tf_op jit(solution)/shard_map/ppermute | solution.py:27
  36.1 4.1 %collective-permute-start.5 = (f32[6,1,4,4,128]{4,3,2,1,0:T(4,128)S(1)}, f32[6,1,4,4,128]{4,3,2,1,0:T(4,128)S(1)}, u32[]{:S(2)}, u32[]{:S(2)}) collective-permute-start(f32[6,1,4,4,128]{4,3,2,1,0:T(4,128)S(1)} %collective-permute-done.4), channel_id=1, source_target_pairs={{0,16},{8,24},{16,0},{24,8},{1,17},{9,25},{17,1},{25,9},{2,18},{10... | collective-permute-start | bytes 147464 | tf_op jit(solution)/shard_map/ppermute | solution.py:27
  40.2 6.1 %collective-permute-start.9 = (f32[6,6,1,4,128]{4,3,2,1,0:T(4,128)S(1)}, f32[6,6,1,4,128]{4,3,2,1,0:T(4,128)S(1)}, u32[]{:S(2)}, u32[]{:S(2)}) collective-permute-start(f32[6,6,1,4,128]{4,3,2,1,0:T(4,128)S(1)} %get-tuple-element.10), channel_id=1, source_target_pairs={{0,4},{2,6},{4,0},{6,2},{1,5},{3,7},{5,1},{7,3},{8,12},{10,14},{12... | collective-permute-start | bytes 221192 | tf_op jit(solution)/shard_map/ppermute | solution.py:27
  43.1 6.1 %collective-permute-start.8 = (f32[6,6,1,4,128]{4,3,2,1,0:T(4,128)S(1)}, f32[6,6,1,4,128]{4,3,2,1,0:T(4,128)S(1)}, u32[]{:S(2)}, u32[]{:S(2)}) collective-permute-start(f32[6,6,1,4,128]{4,3,2,1,0:T(4,128)S(1)} %get-tuple-element.9), channel_id=1, source_target_pairs={{0,4},{2,6},{4,0},{6,2},{1,5},{3,7},{5,1},{7,3},{8,12},{10,14},{12... | collective-permute-start | bytes 221192 | tf_op jit(solution)/shard_map/ppermute | solution.py:27
  49.2 0.8 copy-start
  49.2 0.8 copy-start.2
  49.4 0.7 copy-start.1
  49.4 0.7 copy-start.3

commit v2 on v1

--- a/solution.py
+++ b/solution.py
@@ -19,12 +19,6 @@
 
 SOFTEN = 0.0025
 EXACT_DOTS = lax.Precision.HIGHEST
-
-
-def from_partner(value, axis, stride):
-    mask = 2**stride
-    pairs = [(source, source ^ mask) for source in range(lax.axis_size(axis))]
-    return lax.ppermute(value, axis, pairs)
 
 
 def iota(shape, dimension):
@@ -68,7 +62,9 @@
     dens = jnp.dot(
         up_ref[...], check, preferred_element_type=jnp.float32, precision=EXACT_DOTS
     )
-    dens_ref[...] = jnp.transpose(dens)[:LEAF]
+    dens = jnp.transpose(jnp.concatenate([dens, dens], axis=0))
+    for n in range(LEAF):
+        dens_ref[n] = dens[n : n + 1]
 
 
 def squares_of(points, shift_x, shift_y, shift_z, extra):
@@ -108,11 +104,7 @@
     return jnp.transpose(jnp.concatenate(rows, axis=0)).astype(jnp.bfloat16)
 
 
-def translate_part(dens_ref, inner_ref, down_ref, wide, grouped, local):
-    dens = dens_ref[...]
-    high = rounded(dens)
-    wide[...] = jnp.concatenate([high, rounded(dens - high)], axis=1)
-
+def translate_part(dens_ref, inner_ref, down_ref, grouped, local):
     def clear(n, carry):
         grouped[pl.ds(n * 8, 8)] = jnp.zeros((8, 8, 2 * TERMS), jnp.float32)
         return carry
@@ -129,11 +121,21 @@
                 cell_y = 2 * (parent // 2 % 2) + a_y
                 cell_z = 2 * (parent % 2) + a_z
                 cell = cell_x * 64 + cell_y * 8 + cell_z
-                grouped[to, parent : parent + 1, :] = wide[pl.ds(cell, 1), :]
+                grouped[to, parent : parent + 1, :] = dens_ref[cell]
         return carry
 
     lax.fori_loop(0, 36, gather, 0)
 
+    half = iota((8, 2 * TERMS), 1) < TERMS
+
+    def split(n, carry):
+        at = (n // 36 + 1) * 64 + (n // 6 % 6 + 1) * 8 + n % 6 + 1
+        value = grouped[at]
+        high = rounded(value)
+        grouped[at] = jnp.where(half, high, value - high)
+        return carry
+
+    lax.fori_loop(0, 216, split, 0, unroll=4)
     first = iota((TERMS, 2 * TERMS), 1) < TERMS
     spread = []
     for c in range(3):
@@ -193,14 +195,13 @@
     inner_ref,
     outer_ref,
     out_ref,
-    wide,
     grouped,
     local,
     sources,
     targets,
     surface,
 ):
-    translate_part(dens_ref, inner_ref, down_ref, wide, grouped, local)
+    translate_part(dens_ref, inner_ref, down_ref, grouped, local)
     surface[...] = jnp.zeros((4, PTS), jnp.float32)
     surface[0:3, 0:TERMS] = outer_ref[...]
 
@@ -295,7 +296,7 @@
         upward_body,
         out_shape=(
             jax.ShapeDtypeStruct((LEAF, 4, PTS), jnp.float32),
-            jax.ShapeDtypeStruct((LEAF, TERMS), jnp.float32),
+            jax.ShapeDtypeStruct((LEAF, 1, 2 * TERMS), jnp.float32),
         ),
         in_specs=[whole(), whole(), scalars(), whole(), whole()],
         out_specs=(whole(), whole()),
@@ -310,7 +311,6 @@
         in_specs=[scalars()] + [whole()] * 5,
         out_specs=whole(),
         scratch_shapes=[
-            pltpu.VMEM((512, 2 * TERMS), jnp.float32),
             pltpu.VMEM((512, 8, 2 * TERMS), jnp.float32),
             pltpu.VMEM((LEAF, 2 * TERMS), jnp.float32),
             pltpu.VMEM((EXT + LEAF, FEATS, PTS), jnp.bfloat16),
@@ -329,77 +329,154 @@
     return (low_bits, mid_bits, high_bits)
 
 
-def flip(rising_dens, rising_points, falling_dens, falling_points, global_bit):
+SIDES = [
+    (x, y, z)
+    for x in (-1, 0, 1)
+    for y in (-1, 0, 1)
+    for z in (-1, 0, 1)
+    if (x, y, z) != (0, 0, 0)
+]
+
+
+def rim(side, size, layers):
+    if side > 0:
+        return pl.ds(size - layers, layers), pl.ds(0, layers)
+    if side < 0:
+        return pl.ds(0, layers), pl.ds(size + layers, layers)
+    return pl.ds(0, size), pl.ds(layers, size)
+
+
+def exchange_body(points_ref, dens_ref, wide_points, wide_dens, send_sem, recv_sem):
     low_bits, mid_bits, high_bits = axis_bits()
-    if global_bit < low_bits:
-        return from_partner(
-            (rising_dens, rising_points, falling_dens, falling_points), "gz", global_bit
+    total_bits = low_bits + mid_bits + high_bits
+    device = (
+        lax.axis_index("gx") * 2**mid_bits + lax.axis_index("gy")
+    ) * 2**low_bits + lax.axis_index("gz")
+    place = []
+    extent = []
+    for c in range(3):
+        bits = list(range(c, total_bits, 3))
+        place.append(sum((device // 2**bit % 2) * 2**rank for rank, bit in enumerate(bits)))
+        extent.append(2 ** len(bits))
+
+    def there(side):
+        inside = jnp.bool_(True)
+        for c in range(3):
+            if side[c] > 0:
+                inside = inside & (place[c] < extent[c] - 1)
+            if side[c] < 0:
+                inside = inside & (place[c] > 0)
+        return inside
+
+    def coordinates(side):
+        other = 0
+        for c in range(3):
+            moved = place[c] + side[c]
+            for rank, bit in enumerate(range(c, total_bits, 3)):
+                other = other + (moved // 2**rank % 2) * 2**bit
+        return (
+            other // 2 ** (low_bits + mid_bits),
+            other // 2**low_bits % 2**mid_bits,
+            other % 2**low_bits,
         )
-    if global_bit < low_bits + mid_bits:
-        return from_partner(
-            (rising_dens, rising_points, falling_dens, falling_points), "gy", global_bit - low_bits
-        )
-    return from_partner(
-        (rising_dens, rising_points, falling_dens, falling_points),
-        "gx",
-        global_bit - low_bits - mid_bits,
-    )
-
-
-def box_place(device, dimension, total_bits):
-    place = jnp.zeros((), jnp.int32)
-    for bit_rank, global_bit in enumerate(range(dimension, total_bits, 3)):
-        place = place + jnp.left_shift(
-            jnp.bitwise_and(jnp.right_shift(device, global_bit), 1), bit_rank
-        )
-    return place
-
-
-def extend(density, points, dimension, layers, device, total_bits):
-    position = box_place(device, dimension, total_bits)
-    dens_size = density.shape[dimension]
-    point_size = points.shape[dimension]
-    rising_dens = lax.slice_in_dim(density, dens_size - layers, dens_size, axis=dimension)
-    rising_points = lax.slice_in_dim(points, point_size - 1, point_size, axis=dimension)
-    falling_dens = lax.slice_in_dim(density, 0, layers, axis=dimension)
-    falling_points = lax.slice_in_dim(points, 0, 1, axis=dimension)
-    lower_dens = jnp.zeros_like(rising_dens)
-    lower_points = jnp.zeros_like(rising_points)
-    upper_dens = jnp.zeros_like(falling_dens)
-    upper_points = jnp.zeros_like(falling_points)
-    carried = (rising_dens, rising_points, falling_dens, falling_points)
-    for bit_rank, global_bit in enumerate(range(dimension, total_bits, 3)):
-        carried = flip(carried[0], carried[1], carried[2], carried[3], global_bit)
-        got_lower = (carried[0], carried[1])
-        got_upper = (carried[2], carried[3])
-        bit_value = jnp.bitwise_and(jnp.right_shift(position, bit_rank), 1)
-        below_bits = jnp.bitwise_and(position, (1 << bit_rank) - 1)
-        from_lower = (bit_value == 1) & (below_bits == 0)
-        from_upper = (bit_value == 0) & (below_bits == (1 << bit_rank) - 1)
-        lower_dens = jnp.where(from_lower, got_lower[0], lower_dens)
-        lower_points = jnp.where(from_lower, got_lower[1], lower_points)
-        upper_dens = jnp.where(from_upper, got_upper[0], upper_dens)
-        upper_points = jnp.where(from_upper, got_upper[1], upper_points)
-    density = jnp.concatenate([lower_dens, density, upper_dens], axis=dimension)
-    points = jnp.concatenate([lower_points, points, upper_points], axis=dimension)
-    return (density, points)
+
+    def copies(at):
+        side = SIDES[at]
+        sizes = (CX, CY, CZ)
+        result = []
+        for kind, (own, wide, layers) in enumerate(
+            ((dens_ref, wide_dens, 2), (points_ref, wide_points, 1))
+        ):
+            source, target = zip(*(rim(side[c], sizes[c], layers) for c in range(3)))
+            result.append(
+                pltpu.make_async_remote_copy(
+                    src_ref=own.at[source],
+                    dst_ref=wide.at[target],
+                    send_sem=send_sem.at[kind, at],
+                    recv_sem=recv_sem.at[kind, at],
+                    device_id=coordinates(side),
+                    device_id_type=pl.DeviceIdType.MESH,
+                )
+            )
+        return result
+
+    def clear(n, carry):
+        wide_points[n] = jnp.zeros(wide_points.shape[1:], jnp.float32)
+        return carry
+
+    def clear_dens(n, carry):
+        wide_dens[n] = jnp.zeros(wide_dens.shape[1:], jnp.float32)
+        return carry
+
+    lax.fori_loop(0, CX + 2, clear, 0)
+    lax.fori_loop(0, CX + 4, clear_dens, 0)
+    barrier = pltpu.get_barrier_semaphore()
+    met = jnp.int32(0)
+    for side in SIDES:
+        inside = there(side)
+        met = met + jnp.where(inside, 1, 0)
+
+        @pl.when(inside)
+        def _(side=side):
+            pl.semaphore_signal(
+                barrier,
+                inc=1,
+                device_id=coordinates(side),
+                device_id_type=pl.DeviceIdType.MESH,
+            )
+
+    pl.semaphore_wait(barrier, met)
+    order = sorted(range(len(SIDES)), key=lambda at: sum(map(abs, SIDES[at])))
+    for at in order:
+
+        @pl.when(there(SIDES[at]))
+        def _(at=at):
+            for copy in copies(at):
+                copy.start()
+
+    for x in range(CX):
+        wide_points[x + 1, 1 : CY + 1, 1 : CZ + 1] = points_ref[x]
+        wide_dens[x + 2, 2 : CY + 2, 2 : CZ + 2] = dens_ref[x]
+    for at in order:
+
+        @pl.when(there(SIDES[at]))
+        def _(at=at):
+            for copy in copies(at):
+                copy.wait_send()
+
+        @pl.when(there(tuple(-c for c in SIDES[at])))
+        def _(at=at):
+            for copy in copies(at):
+                copy.wait_recv()
+
+
+def exchange(points, density):
+    return pl.pallas_call(
+        exchange_body,
+        out_shape=(
+            jax.ShapeDtypeStruct((CX + 2, CY + 2, CZ + 2, 4, PTS), jnp.float32),
+            jax.ShapeDtypeStruct((CX + 4, CY + 4, CZ + 4, 1, 2 * TERMS), jnp.float32),
+        ),
+        in_specs=[whole(), whole()],
+        out_specs=(whole(), whole()),
+        scratch_shapes=[
+            pltpu.SemaphoreType.DMA((2, len(SIDES))),
+            pltpu.SemaphoreType.DMA((2, len(SIDES))),
+        ],
+        compiler_params=pltpu.CompilerParams(collective_id=0, has_side_effects=True),
+        name="exchange",
+    )(points, density)
 
 
 def per_device(positions, charges, counts, up_inverse, down_inverse, inner_surface, outer_surface):
     point_flat, density = upward(positions, charges, counts, up_inverse, outer_surface)
-    dens_grid = density.reshape(CX, CY, CZ, TERMS)
-    point_grid = point_flat.reshape(CX, CY, CZ, 4, PTS)
-    low_bits, mid_bits, high_bits = axis_bits()
-    total_bits = low_bits + mid_bits + high_bits
-    device = (lax.axis_index("gx") * lax.axis_size("gy") + lax.axis_index("gy")) * lax.axis_size(
-        "gz"
-    ) + lax.axis_index("gz")
-    for dimension in range(3):
-        dens_grid, point_grid = extend(dens_grid, point_grid, dimension, 2, device, total_bits)
+    point_grid, dens_grid = exchange(
+        point_flat.reshape(CX, CY, CZ, 4, PTS), density.reshape(CX, CY, CZ, 1, 2 * TERMS)
+    )
     return potentials(
         counts,
         point_grid.reshape(EXT, 4, PTS),
-        dens_grid.reshape(512, TERMS),
+        dens_grid.reshape(512, 1, 2 * TERMS),
         down_inverse,
         inner_surface,
         outer_surface,

time: 99 us -> 77.7 us (0.78)
  waiting for transfers between devices: 21.5 us -> 0 us
  Pallas kernels: 52.8 us -> 72.8 us
  starting transfers between devices: 19.9 us -> 0 us
    ppermute x20 -> x0, waiting for transfers between devices: 21.5 us -> none  [from_partner(): return lax.ppermute(value, axis, pairs)]
    ppermute x20 -> x0, starting transfers between devices: 19.9 us -> none  [from_partner(): return lax.ppermute(value, axis, pairs)]
    pallas_call x0 -> x1, Pallas kernels: none -> 16.7 us  [exchange(): pl.pallas_call(exchange_body, out_shape=(jax.ShapeDtypeStruct((CX + 2, CY...]
    pallas_call x1, Pallas kernels: 48.8 us -> 52 us  [potentials(): pl.pallas_call(near_body, out_shape=jax.ShapeDtypeStruct((LEAF, PTS), jnp...]
    unnamed x13, local copies, waits for them, and re-layouts: 2.3 us -> 4.25 us
    slice x4 -> x0, local copies, waits for them, and re-layouts: 1.58 us -> none  [the longest x3 0.8 us: extend(): lax.slice_in_dim(density, dens_size - layers, dens_size, axis=dimension)]
  transfers between devices with their start and end apart: 20 -> 0, of which waited for: 11 -> 0; matrix products, arithmetic and copies ran while one was open for 1% -> 0% of each run, Pallas kernels for 0% -> 0%
where the time goes in v2:
time: 77.7 us; the launch traced here: 77.1 us
  Pallas kernels  72.8 us (94%)
  local copies, waits for them, and re-layouts  4.25 us (5%)
    pallas_call x1, Pallas kernels, potentials(): pl.pallas_call(near_body, out_shape=jax.ShapeDtypeStruct((LEAF, PTS), jnp...  52 us
    pallas_call x1, Pallas kernels, exchange(): pl.pallas_call(exchange_body, out_shape=(jax.ShapeDtypeStruct((CX + 2, CY...  16.7 us
    unnamed x13, local copies, waits for them, and re-layouts  4.25 us
    pallas_call x1, Pallas kernels, upward(): pl.pallas_call(upward_body, out_shape=(jax.ShapeDtypeStruct((LEAF, 4, PTS...  4.06 us

profile of v2, /device:TPU:0, one launch (start us, length us, event | category | flops | bytes accessed | tf_op | source)
XLA Modules:
  0.0 77.1 jit_solution(11426657934483024882)
XLA Ops:
  0.0 1.6 %copy.8.pos_ref = f32[64,3,128]{2,1,0:T(4,128)} copy(f32[64,3,128]{2,0,1:T(8,128)} %param.7) | data formatting | bytes 196608 | tf_op args[0]
  1.6 4.1 %upward.1 = (f32[64,4,128]{2,1,0:T(4,128)}, f32[64,1,128]{2,1,0:T(1,128)}) custom-call(f32[64,3,128]{2,1,0:T(4,128)} %copy.8.pos_ref, f32[64,128]{1,0:T(8,128)} %charge_ref.1, s32[64]{0:T(128)} %count_ref.3, f32[64,64]{1,0:T(8,128)} %up_ref.1, f32[3,64]{1,0:T(4,128)} %outer_ref.3), custom_call_target="tpu_custom_call" | custom-call | tf_op jit(solution)/shard_map/upward/pallas_call | solution.py:295
  5.7 0.0 copy-start.2
  5.7 16.7 %exchange.1 = (f32[6,6,6,4,128]{4,3,2,1,0:T(4,128)}, f32[8,8,8,1,128]{4,3,2,1,0:T(1,128)}) custom-call(f32[4,4,4,4,128]{4,3,2,1,0:T(4,128)} %bitcast.6, f32[4,4,4,1,128]{4,3,2,1,0:T(1,128)} %bitcast.7), custom_call_target="tpu_custom_call" | custom-call | tf_op jit(solution)/shard_map/exchange/pallas_call | solution.py:454
  22.4 0.0 copy-start.4
  22.4 0.0 copy-start.3
  22.4 0.0 copy-start.5
  22.4 0.0 copy-done.2
  22.4 0.6 copy-done.4
  23.1 0.0 copy-done.3
  23.1 0.0 copy-done.5
  23.1 0.0 copy-start
  23.1 1.0 %copy-done = f32[6,6,6,4,128]{4,3,2,1,0:T(4,128)S(1)} copy-done((f32[6,6,6,4,128]{4,3,2,1,0:T(4,128)S(1)}, f32[6,6,6,4,128]{4,3,2,1,0:T(4,128)}, u32[]{:S(2)}) %copy-start) | copy-done | bytes 442392
  24.1 0.0 copy-start.1
  24.1 0.9 %copy-done.1 = f32[8,8,8,1,128]{4,3,2,1,0:T(1,128)S(1)} copy-done((f32[8,8,8,1,128]{4,3,2,1,0:T(1,128)S(1)}, f32[8,8,8,1,128]{4,3,2,1,0:T(1,128)}, u32[]{:S(2)}) %copy-start.1) | copy-done | bytes 262168
  25.1 52.0 %potentials.1 = f32[64,128]{1,0:T(8,128)} custom-call(s32[64]{0:T(128)S(1)} %copy-done.5, f32[216,4,128]{2,1,0:T(4,128)S(1)} %bitcast.4, f32[512,1,128]{2,1,0:T(1,128)S(1)} %bitcast.5, f32[64,64]{1,0:T(8,128)S(1)} %copy-done.2, f32[3,64]{1,0:T(4,128)S(1)} %copy-done.4, f32[3,64]{1,0:T(4,128)S(1)} %copy-done.3), custom_call_target="tpu_custom_call" | custom-call | tf_op jit(solution)/shard_map/potentials/pallas_call | solution.py:308
Async XLA Ops:
  5.7 16.8 %copy-start.2 = (f32[64,64]{1,0:T(8,128)S(1)}, f32[64,64]{1,0:T(8,128)}, u32[]{:S(2)}) copy-start(f32[64,64]{1,0:T(8,128)} %down_ref.1) | copy-start | bytes 49156
  22.4 0.7 copy-start.4
  22.4 0.7 copy-start.3
  22.4 0.7 copy-start.5
  23.1 1.0 %copy-start = (f32[6,6,6,4,128]{4,3,2,1,0:T(4,128)S(1)}, f32[6,6,6,4,128]{4,3,2,1,0:T(4,128)}, u32[]{:S(2)}) copy-start(f32[6,6,6,4,128]{4,3,2,1,0:T(4,128)} %get-tuple-element.11) | copy-start | bytes 1327108
  24.1 0.9 %copy-start.1 = (f32[8,8,8,1,128]{4,3,2,1,0:T(1,128)S(1)}, f32[8,8,8,1,128]{4,3,2,1,0:T(1,128)}, u32[]{:S(2)}) copy-start(f32[8,8,8,1,128]{4,3,2,1,0:T(1,128)} %get-tuple-element.12) | copy-start | bytes 786436

commit v3 on v2

--- a/solution.py
+++ b/solution.py
@@ -15,6 +15,7 @@
 LEAF = CX * CY * CZ
 EXT = (CX + 2) * (CY + 2) * (CZ + 2)
 FEATS = 32
+LINE = 4
 
 
 SOFTEN = 0.0025
@@ -29,6 +30,13 @@
     size = row.shape[1]
     eye = iota((size, size), 0) == iota((size, size), 1)
     return jnp.sum(jnp.where(eye, row, 0.0), axis=1, keepdims=True)
+
+
+def over_plane(size_x, size_y, body, start, unroll=1):
+    def line(x, carry):
+        return lax.fori_loop(0, size_y, lambda y, held: body(x, y, held), carry, unroll=unroll)
+
+    return lax.fori_loop(0, size_x, line, start)
 
 
 def rounded(value):
@@ -111,9 +119,7 @@
 
     lax.fori_loop(0, 64, clear, 0)
 
-    def gather(n, carry):
-        a_x = n // 6
-        a_y = n % 6
+    def gather(a_x, a_y, carry):
         for a_z in range(6):
             to = (a_x + 1) * 64 + (a_y + 1) * 8 + a_z + 1
             for parent in range(8):
@@ -124,27 +130,28 @@
                 grouped[to, parent : parent + 1, :] = dens_ref[cell]
         return carry
 
-    lax.fori_loop(0, 36, gather, 0)
+    over_plane(6, 6, gather, 0, 6)
 
     half = iota((8, 2 * TERMS), 1) < TERMS
 
-    def split(n, carry):
-        at = (n // 36 + 1) * 64 + (n // 6 % 6 + 1) * 8 + n % 6 + 1
-        value = grouped[at]
-        high = rounded(value)
-        grouped[at] = jnp.where(half, high, value - high)
-        return carry
-
-    lax.fori_loop(0, 216, split, 0, unroll=4)
+    def split(a_x, a_y, carry):
+        for a_z in range(6):
+            at = (a_x + 1) * 64 + (a_y + 1) * 8 + a_z + 1
+            value = grouped[at]
+            high = rounded(value)
+            grouped[at] = jnp.where(half, high, value - high)
+        return carry
+
+    over_plane(6, 6, split, 0, 6)
     first = iota((TERMS, 2 * TERMS), 1) < TERMS
     spread = []
     for c in range(3):
         row = inner_ref[c : c + 1, :]
         spread.append(jnp.concatenate([row, row], axis=1) - column(row))
 
-    def shift_pair(n, total):
-        shift_x = n // 7 - 3
-        shift_y = n % 7 - 3
+    def shift_pair(n_x, n_y, total):
+        shift_x = n_x - 3
+        shift_y = n_y - 3
         d_x = spread[0] - shift_x.astype(jnp.float32)
         d_y = spread[1] - shift_y.astype(jnp.float32)
         plane = d_x * d_x + d_y * d_y + SOFTEN
@@ -174,7 +181,7 @@
             total = total + jnp.dot(left, right, preferred_element_type=jnp.float32)
         return total
 
-    total = lax.fori_loop(0, 49, shift_pair, jnp.zeros((LEAF, 2 * TERMS), jnp.float32))
+    total = over_plane(7, 7, shift_pair, jnp.zeros((LEAF, 2 * TERMS), jnp.float32), 7)
     down = down_ref[...]
     down = jnp.concatenate([down, down], axis=1)
     down = jnp.concatenate([down, jnp.zeros_like(down)], axis=0)
@@ -206,41 +213,38 @@
     surface[0:3, 0:TERMS] = outer_ref[...]
 
     def middle(cell):
-        return cell.astype(jnp.float32) - (CX // 2 + 1)
-
-    def prepare(n, carry):
-        e_x = n // ((CY + 2) * (CZ + 2))
-        e_y = n // (CZ + 2) % (CY + 2)
-        e_z = n % (CZ + 2)
-        sources[n] = source_features(points_ref[n], middle(e_x), middle(e_y), middle(e_z))
-        return carry
-
-    lax.fori_loop(0, EXT, prepare, 0, unroll=4)
-
-    def ext_index(n):
-        return (n // (CY * CZ) + 1) * ((CY + 2) * (CZ + 2)) + (n // CZ % CY + 1) * (CZ + 2) + (
-            n % CZ + 1
+        return jnp.float32(cell) - (CX // 2 + 1) if isinstance(cell, int) else (
+            cell.astype(jnp.float32) - (CX // 2 + 1)
         )
 
-    def prepare_own(n, carry):
-        x = middle(n // (CY * CZ) + 1)
-        y = middle(n // CZ % CY + 1)
-        z = middle(n % CZ + 1)
-        targets[n] = target_features(points_ref[ext_index(n)], x, y, z)
-        sources[EXT + n] = source_features(surface[...], x, y, z)
-        return carry
-
-    lax.fori_loop(0, LEAF, prepare_own, 0, unroll=4)
+    def prepare(e_x, e_y, carry):
+        for e_z in range(CZ + 2):
+            n = (e_x * (CY + 2) + e_y) * (CZ + 2) + e_z
+            sources[n] = source_features(points_ref[n], middle(e_x), middle(e_y), middle(e_z))
+        return carry
+
+    over_plane(CX + 2, CY + 2, prepare, 0, CY + 2)
+
+    def ext_index(x, y, z):
+        return ((x + 1) * (CY + 2) + y + 1) * (CZ + 2) + z + 1
+
+    def prepare_own(x, y, carry):
+        for z in range(CZ):
+            n = (x * CY + y) * CZ + z
+            place = (middle(x + 1), middle(y + 1), middle(z + 1))
+            targets[n] = target_features(points_ref[ext_index(x, y, z)], *place)
+            sources[EXT + n] = source_features(surface[...], *place)
+        return carry
+
+    over_plane(CX, CY, prepare_own, 0, CY)
 
     lane = iota((1, PTS), 1)
 
-    def leaf(n, carry):
-        base = ext_index(n)
-        x = n // (CY * CZ)
-        y = n // CZ % CY
-        z = n % CZ
-        parity = (x % 2) * 4 + (y % 2) * 2 + z % 2
-        parent = (x // 2) * 4 + (y // 2) * 2 + z // 2
+    def leaf(x, y, z):
+        n = (x * CY + y) * CZ + z
+        base = ext_index(x, y, z)
+        parity = (x & 1) * 4 + (y & 1) * 2 + (z & 1)
+        parent = (x >> 1) * 4 + (y >> 1) * 2 + (z >> 1)
         count = count_ref[n]
         blocks = []
         for s_x in range(-1, 2):
@@ -275,12 +279,30 @@
             flat = jnp.sum(jnp.where(eye, sums, 0.0), axis=0, keepdims=True)
             out_ref[pl.ds(n, 1), :] = jnp.where(lane < count, flat, 0.0)
 
-        filled = (count + 31) // 32
+        return (count + 31) >> 5, rows
+
+    def leaf_group(x, y, z):
+        group = [leaf(x, y, z + k) for k in range(LINE)]
+        most = group[0][0]
+        for filled, _ in group[1:]:
+            most = jnp.maximum(most, filled)
+
+        def together(size):
+            for _, rows in group:
+                rows(size)
+
         for k in range(1, 5):
-            pl.when(filled == k)(partial(rows, 32 * k))
-        return carry
-
-    lax.fori_loop(0, LEAF, leaf, 0)
+            pl.when(most == k)(partial(together, 32 * k))
+
+    def leaf_line(x, y, carry):
+        if LINE == CZ:
+            leaf_group(x, y, 0)
+        else:
+            for z in range(0, CZ, LINE):
+                leaf_group(x, y, z)
+        return carry
+
+    over_plane(CX, CY, leaf_line, 0)
 
 
 def whole():

time: 77.7 us -> 53.3 us (0.69)
  Pallas kernels: 72.8 us -> 48.7 us
    pallas_call x1, Pallas kernels: 52 us -> 28 us  [potentials(): pl.pallas_call(near_body, out_shape=jax.ShapeDtypeStruct((LEAF, PTS), jnp...]
where the time goes in v3:
time: 53.3 us; the launch traced here: 53 us
  Pallas kernels  48.7 us (91%)
  local copies, waits for them, and re-layouts  4.25 us (8%)
    pallas_call x1, Pallas kernels, potentials(): pl.pallas_call(near_body, out_shape=jax.ShapeDtypeStruct((LEAF, PTS), jnp...  28 us
    pallas_call x1, Pallas kernels, exchange(): pl.pallas_call(exchange_body, out_shape=(jax.ShapeDtypeStruct((CX + 2, CY...  16.7 us
    unnamed x13, local copies, waits for them, and re-layouts  4.25 us
    pallas_call x1, Pallas kernels, upward(): pl.pallas_call(upward_body, out_shape=(jax.ShapeDtypeStruct((LEAF, 4, PTS...  4.06 us

profile of v3, /device:TPU:0, one launch (start us, length us, event | category | flops | bytes accessed | tf_op | source)
XLA Modules:
  0.0 53.0 jit_solution(1817812912940264880)
XLA Ops:
  0.0 1.6 %copy.8.pos_ref = f32[64,3,128]{2,1,0:T(4,128)} copy(f32[64,3,128]{2,0,1:T(8,128)} %param.7) | data formatting | bytes 196608 | tf_op args[0]
  1.6 4.1 %upward.1 = (f32[64,4,128]{2,1,0:T(4,128)}, f32[64,1,128]{2,1,0:T(1,128)}) custom-call(f32[64,3,128]{2,1,0:T(4,128)} %copy.8.pos_ref, f32[64,128]{1,0:T(8,128)} %charge_ref.1, s32[64]{0:T(128)} %count_ref.3, f32[64,64]{1,0:T(8,128)} %up_ref.1, f32[3,64]{1,0:T(4,128)} %outer_ref.3), custom_call_target="tpu_custom_call" | custom-call | tf_op jit(solution)/shard_map/upward/pallas_call | solution.py:317
  5.7 0.0 copy-start.2
  5.7 16.7 %exchange.1 = (f32[6,6,6,4,128]{4,3,2,1,0:T(4,128)}, f32[8,8,8,1,128]{4,3,2,1,0:T(1,128)}) custom-call(f32[4,4,4,4,128]{4,3,2,1,0:T(4,128)} %bitcast.6, f32[4,4,4,1,128]{4,3,2,1,0:T(1,128)} %bitcast.7), custom_call_target="tpu_custom_call" | custom-call | tf_op jit(solution)/shard_map/exchange/pallas_call | solution.py:476
  22.4 0.0 copy-start.4
  22.4 0.0 copy-start.3
  22.4 0.0 copy-start.5
  22.4 0.0 copy-done.2
  22.4 0.6 %copy-done.4 = f32[3,64]{1,0:T(4,128)S(1)} copy-done((f32[3,64]{1,0:T(4,128)S(1)}, f32[3,64]{1,0:T(4,128)}, u32[]{:S(2)}) %copy-start.4) | copy-done | bytes 792
  23.1 0.0 copy-done.3
  23.1 0.0 copy-done.5
  23.1 0.0 copy-start
  23.1 1.0 %copy-done = f32[6,6,6,4,128]{4,3,2,1,0:T(4,128)S(1)} copy-done((f32[6,6,6,4,128]{4,3,2,1,0:T(4,128)S(1)}, f32[6,6,6,4,128]{4,3,2,1,0:T(4,128)}, u32[]{:S(2)}) %copy-start) | copy-done | bytes 442392
  24.1 0.0 copy-start.1
  24.1 0.9 %copy-done.1 = f32[8,8,8,1,128]{4,3,2,1,0:T(1,128)S(1)} copy-done((f32[8,8,8,1,128]{4,3,2,1,0:T(1,128)S(1)}, f32[8,8,8,1,128]{4,3,2,1,0:T(1,128)}, u32[]{:S(2)}) %copy-start.1) | copy-done | bytes 262168
  25.1 28.0 %potentials.1 = f32[64,128]{1,0:T(8,128)} custom-call(s32[64]{0:T(128)S(1)} %copy-done.5, f32[216,4,128]{2,1,0:T(4,128)S(1)} %bitcast.4, f32[512,1,128]{2,1,0:T(1,128)S(1)} %bitcast.5, f32[64,64]{1,0:T(8,128)S(1)} %copy-done.2, f32[3,64]{1,0:T(4,128)S(1)} %copy-done.4, f32[3,64]{1,0:T(4,128)S(1)} %copy-done.3), custom_call_target="tpu_custom_call" | custom-call | tf_op jit(solution)/shard_map/potentials/pallas_call | solution.py:330
Async XLA Ops:
  5.7 16.8 %copy-start.2 = (f32[64,64]{1,0:T(8,128)S(1)}, f32[64,64]{1,0:T(8,128)}, u32[]{:S(2)}) copy-start(f32[64,64]{1,0:T(8,128)} %down_ref.1) | copy-start | bytes 49156
  22.4 0.7 %copy-start.4 = (f32[3,64]{1,0:T(4,128)S(1)}, f32[3,64]{1,0:T(4,128)}, u32[]{:S(2)}) copy-start(f32[3,64]{1,0:T(4,128)} %inner_ref.1) | copy-start | bytes 2308
  22.4 0.7 %copy-start.3 = (f32[3,64]{1,0:T(4,128)S(1)}, f32[3,64]{1,0:T(4,128)}, u32[]{:S(2)}) copy-start(f32[3,64]{1,0:T(4,128)} %outer_ref.3) | copy-start | bytes 2308
  22.4 0.7 %copy-start.5 = (s32[64]{0:T(128)S(1)}, s32[64]{0:T(128)}, u32[]{:S(2)}) copy-start(s32[64]{0:T(128)} %count_ref.3) | copy-start | bytes 772
  23.1 1.0 %copy-start = (f32[6,6,6,4,128]{4,3,2,1,0:T(4,128)S(1)}, f32[6,6,6,4,128]{4,3,2,1,0:T(4,128)}, u32[]{:S(2)}) copy-start(f32[6,6,6,4,128]{4,3,2,1,0:T(4,128)} %get-tuple-element.11) | copy-start | bytes 1327108
  24.1 0.9 %copy-start.1 = (f32[8,8,8,1,128]{4,3,2,1,0:T(1,128)S(1)}, f32[8,8,8,1,128]{4,3,2,1,0:T(1,128)}, u32[]{:S(2)}) copy-start(f32[8,8,8,1,128]{4,3,2,1,0:T(1,128)} %get-tuple-element.12) | copy-start | bytes 786436
